TPU v7x, 32 devices: a whole 2x2x4 slice. The times are simulated.
32 devices in a mesh: bx: 8 (over y, x, core), by: 4 (over z).
Axes of the slice: x: 2, y: 2, z: 4, core: 2. Of those that a mesh axis runs over, the one named last changes fastest.
Arguments:
- interface_velocity: float32 [3, 2048, 2048], P(None, 'bx', 'by'), may hold values from -6 to 6
- history: float32 [6, 2, 3, 256, 8, 4, 512], P(None, None, None, 'by', 'bx'), may hold values from -6 to 6
- kernel: float32 [7, 256, 8, 4, 512], P(None, 'by', 'bx'), may hold values from -6 to 6
- velocity: float32 [3, 4, 2048, 2048], P(None, None, 'bx', 'by'), may hold values from -6 to 6
- stress: float32 [6, 4, 2048, 2048], P(None, None, 'bx', 'by'), may hold values from -6 to 6
- cohesion: float32 [4, 2048, 2048], P(None, 'bx', 'by'), may hold values from 0.5 to 4
Outputs:
- velocity_new: float32 [3, 4, 2048, 2048], P(None, None, 'bx', 'by')
- stress_new: float32 [6, 4, 2048, 2048], P(None, None, 'bx', 'by')
All inputs are finite; a program needn't handle non-finite values.
Results may differ from a plain program's by a relative error of at most 0.00005.
Values sent between devices are 32-bit elements; how exact they have to be, the bound alone decides.
A program may use at most 192 MiB of HBM per device.

v0:
```python
from functools import partial
import math

import jax
import jax.numpy as jnp
from jax import lax
from jax.sharding import PartitionSpec as P

COURANT = 0.3
FRICTION = 0.6
HIGHEST = lax.Precision.HIGHEST


def extended(block, sides, width):
    for axis, dim in sides:
        count = lax.axis_size(axis)
        forward = [(i, i + 1) for i in range(count - 1)]
        forward.append((count - 1, 0))
        backward = [(target, source) for source, target in forward]
        low = lax.ppermute(
            lax.slice_in_dim(block, block.shape[dim] - width, None, axis=dim), axis, forward
        )
        high = lax.ppermute(lax.slice_in_dim(block, 0, width, axis=dim), axis, backward)
        block = jnp.concatenate([low, block, high], axis=dim)
    return block


def counting(count):
    return jnp.arange(count, dtype=jnp.int32)


def phase_table(row_index, col_index, length, sign):
    product = row_index[:, None] * col_index[None, :] % length
    angle = 2.0 * math.pi / length * product.astype(jnp.float32)
    return (jnp.cos(angle), sign * jnp.sin(angle))


def conjugate(table):
    return (table[0], -table[1])


def complex_apply(pattern, real_part, imag_part, table):
    contract = partial(jnp.einsum, pattern, precision=HIGHEST)
    return (
        contract(real_part, table[0]) - contract(imag_part, table[1]),
        contract(real_part, table[1]) + contract(imag_part, table[0]),
    )


def twist(real_part, imag_part, table_real, table_imag):
    return (
        real_part * table_real - imag_part * table_imag,
        real_part * table_imag + imag_part * table_real,
    )


def plane_blocks(block):
    return lax.all_to_all(block, "bx", split_axis=2, concat_axis=2, tiled=True)


def dip_blocks(block):
    return lax.all_to_all(block, "by", split_axis=2, concat_axis=2, tiled=True)


def strike_modes(block):
    return lax.all_to_all(block, "bx", split_axis=4, concat_axis=4, tiled=True)


def widen(fields):
    return extended(fields, (("bx", 2), ("by", 3)), 1)


def strike_diff(padded):
    return 0.5 * (padded[..., 2:, 1:-1] - padded[..., :-2, 1:-1])


def dip_diff(padded):
    return 0.5 * (padded[..., 1:-1, 2:] - padded[..., 1:-1, :-2])


def depth_diff(layered, ghost_layer):
    above_layer = jnp.concatenate([layered[1:], jnp.zeros_like(layered[:1])], axis=0)
    below_layer = jnp.concatenate([ghost_layer[None], layered[:-1]], axis=0)
    return 0.5 * (above_layer - below_layer)


def yield_limit(trial_stress, cohesion):
    pressure = (trial_stress[0] + trial_stress[1] + trial_stress[2]) / 3.0
    normal_dev = trial_stress[:3] - pressure[None]
    second = 0.5 * jnp.sum(normal_dev * normal_dev, axis=0) + jnp.sum(
        trial_stress[3:] * trial_stress[3:], axis=0
    )
    shear_stress = jnp.sqrt(second)
    yield_stress = cohesion + FRICTION * jnp.maximum(-pressure, 0.0)
    factor = yield_stress / jnp.maximum(shear_stress, yield_stress)
    return jnp.concatenate(
        [pressure[None] + factor[None] * normal_dev, factor[None] * trial_stress[3:]], axis=0
    )


def advance_bulk(velocity, stress, traction, interface_velocity, cohesion):
    padded_stress = widen(stress)
    forcing = jnp.stack(
        [
            strike_diff(padded_stress[0])
            + dip_diff(padded_stress[3])
            + depth_diff(stress[4], traction[0]),
            strike_diff(padded_stress[3])
            + dip_diff(padded_stress[1])
            + depth_diff(stress[5], traction[1]),
            strike_diff(padded_stress[4])
            + dip_diff(padded_stress[5])
            + depth_diff(stress[2], traction[2]),
        ]
    )
    velocity_new = velocity + COURANT * forcing
    padded_velocity = widen(velocity_new)
    strike_grad = strike_diff(padded_velocity)
    dip_grad = dip_diff(padded_velocity)
    depth_grad = jnp.stack(
        [
            depth_diff(velocity_new[component], interface_velocity[component])
            for component in range(3)
        ]
    )
    dilation = strike_grad[0] + dip_grad[1] + depth_grad[2]
    rates = jnp.stack(
        [
            dilation + 2.0 * strike_grad[0],
            dilation + 2.0 * dip_grad[1],
            dilation + 2.0 * depth_grad[2],
            dip_grad[0] + strike_grad[1],
            depth_grad[0] + strike_grad[2],
            depth_grad[1] + dip_grad[2],
        ]
    )
    trial_stress = stress + COURANT * rates
    return (velocity_new, yield_limit(trial_stress, cohesion))


def local(interface_velocity, history, kernel, velocity, stress, cohesion):
    strike_count = lax.axis_size("bx")
    dip_count = lax.axis_size("by")
    strike_index = lax.axis_index("bx")
    strike_cells = interface_velocity.shape[1]
    dip_cells = interface_velocity.shape[2]
    row_block = dip_cells // strike_count
    mode_block = strike_cells // dip_count
    strike_length = strike_cells * strike_count
    dip_length = dip_cells * dip_count
    scale = 1.0 / math.sqrt(strike_length * dip_length)
    strike_table = phase_table(counting(strike_count), counting(strike_count), strike_count, -1.0)
    strike_twist = phase_table(counting(strike_cells), counting(strike_count), strike_length, -1.0)
    cell_table = phase_table(counting(strike_cells), counting(strike_cells), strike_cells, -1.0)
    dip_table = phase_table(counting(dip_count), counting(dip_count), dip_count, -1.0)
    column_table = phase_table(counting(dip_cells), counting(dip_cells), dip_cells, -1.0)
    grouped = plane_blocks(interface_velocity).reshape(3, strike_cells, strike_count, row_block)
    first_pattern = "cqpr,pk->cqkr"
    real_part = jnp.einsum(first_pattern, grouped, strike_table[0], precision=HIGHEST)
    imag_part = jnp.einsum(first_pattern, grouped, strike_table[1], precision=HIGHEST)
    real_part, imag_part = twist(
        real_part, imag_part, strike_twist[0][None, :, :, None], strike_twist[1][None, :, :, None]
    )
    real_part, imag_part = complex_apply("cqkr,qm->cmkr", real_part, imag_part, cell_table)
    stacked = jnp.stack([real_part, imag_part])
    dip_offsets = row_block * strike_index + counting(row_block)
    dip_twist = phase_table(counting(dip_count), dip_offsets, dip_length, -1.0)
    arrived = dip_blocks(stacked.reshape(2, 3, strike_cells, dip_cells))
    arrived = arrived.reshape(2, 3, dip_count, mode_block, strike_count, row_block)
    real_part, imag_part = complex_apply("cjukr,jl->clukr", arrived[0], arrived[1], dip_table)
    real_part, imag_part = twist(
        real_part,
        imag_part,
        dip_twist[0][None, :, None, None, :],
        dip_twist[1][None, :, None, None, :],
    )
    arrived = strike_modes(
        jnp.stack([real_part, imag_part]).reshape(2, 3, dip_count, mode_block, dip_cells)
    )
    real_part, imag_part = (arrived[0], arrived[1])
    real_part, imag_part = complex_apply("clus,sm->culm", real_part, imag_part, column_table)
    spectrum = scale * jnp.stack([real_part, imag_part])[:, :, :, None]
    past_terms = jnp.einsum("hupks,hzcupks->zcupks", kernel[1:], history, precision=HIGHEST)
    response = kernel[0][None, None] * spectrum + past_terms
    real_part, imag_part = complex_apply(
        "cuks,sm->ckum", response[0, :, :, 0], response[1, :, :, 0], conjugate(column_table)
    )
    dip_offsets = row_block * strike_index + counting(row_block)
    back_twist = conjugate(phase_table(counting(dip_count), dip_offsets, dip_length, -1.0))
    arrived = strike_modes(jnp.stack([real_part, imag_part]))
    arrived = arrived.reshape(2, 3, dip_count, mode_block, strike_count, row_block)
    real_part, imag_part = twist(
        arrived[0],
        arrived[1],
        back_twist[0][None, :, None, None, :],
        back_twist[1][None, :, None, None, :],
    )
    real_part, imag_part = complex_apply(
        "clukr,lj->cjukr", real_part, imag_part, conjugate(dip_table)
    )
    arrived = dip_blocks(jnp.stack([real_part, imag_part]).reshape(2, 3, strike_cells, dip_cells))
    arrived = arrived.reshape(2, 3, strike_cells, strike_count, row_block)
    real_part, imag_part = complex_apply(
        "cmkr,mq->cqkr", arrived[0], arrived[1], conjugate(cell_table)
    )
    back_strike = conjugate(strike_twist)
    real_part, imag_part = twist(
        real_part, imag_part, back_strike[0][None, :, :, None], back_strike[1][None, :, :, None]
    )
    inverse_table = conjugate(strike_table)
    spatial = jnp.einsum(
        "cqkr,kp->cqpr", real_part, inverse_table[0], precision=HIGHEST
    ) - jnp.einsum("cqkr,kp->cqpr", imag_part, inverse_table[1], precision=HIGHEST)
    traction = scale * plane_blocks(spatial.reshape(3, strike_cells, dip_cells))
    velocity_new, stress_new = advance_bulk(
        velocity, stress, traction, interface_velocity, cohesion
    )
    return (velocity_new, stress_new)


def solution(mesh):
    return jax.shard_map(
        local,
        mesh=mesh,
        in_specs=(
            P(None, "bx", "by"),
            P(None, None, None, "by", "bx", None, None),
            P(None, "by", "bx", None, None),
            P(None, None, "bx", "by"),
            P(None, None, "bx", "by"),
            P(None, "bx", "by"),
        ),
        out_specs=(P(None, None, "bx", "by"), P(None, None, "bx", "by")),
        check_vma=False,
    )
```

profile of v0, /device:TPU:0, one launch (start us, length us, event | category | flops | bytes accessed | tf_op | source)
XLA Modules:
  0.0 765.6 jit_solution(9663773815193796683)
XLA Ops:
  8.7 26.5 %all-to-all-done = f32[3,256,512]{1,0,2:T(4,128)S(1)} async-done(((f32[3,256,512]{1,0,2:T(4,128)}), f32[3,256,512]{1,0,2:T(4,128)S(1)}, u32[]{:S(2)}, u32[]{:S(2)}) %all-to-all-start) | async-done | bytes 1572896 | tf_op jit(solution)/shard_map/all_to_all | solution.py:58
  72.4 67.8 %all-to-all-done.1 = f32[2,3,256,512]{3,0,1,2:T(2,128)S(1)} async-done(((f32[2,3,256,512]{3,0,1,2:T(2,128)}), f32[2,3,256,512]{3,0,1,2:T(2,128)S(1)}, u32[]{:S(2)}, u32[]{:S(2)}) %all-to-all-start.1) | async-done | bytes 3145760 | tf_op jit(solution)/shard_map/all_to_all | solution.py:62
  140.3 11.0 %slice_reduce_fusion.1 = (f32[3,256,512]{2,0,1:T(4,128)}, f32[3,256,512]{2,0,1:T(4,128)}) fusion(f32[2,3,256,512]{3,0,1,2:T(2,128)S(1)} %all-to-all-done.1), kind=kLoop, calls=%fused_computation.117 | loop fusion | bytes 6291456 | tf_op jit(solution)/shard_map/slice | solution.py:170
  154.3 7.6 fusion.8
  161.9 7.5 fusion.10
  172.9 8.1 %fusion.41 = f32[4,3,64,8,64]{4,0,3,2,1:T(4,128)S(1)} fusion(f32[4,3,64,8,64]{4,0,3,2,1:T(4,128)} %fusion.8, f32[3,4,64,8,64]{4,3,0,2,1:T(8,128)S(1)} %reshape.269), kind=kOutput, calls=%fused_computation.113 | convolution fusion | flops 19267824 | bytes 4718592 | tf_op jit(solution)/shard_map/cjukr,jl->clukr/dot_general | solution.py:46
  181.0 9.6 %subtract_bitcast_fusion.1 = (f32[3,4,64,8,64]{4,1,3,2,0:T(4,128)S(1)}, f32[3,4,64,8,64]{4,1,3,2,0:T(4,128)}) fusion(f32[4,3,64,8,64]{4,0,3,2,1:T(4,128)S(1)} %fusion.41, f32[4,64]{1,0:T(4,128)S(1)} %get-tuple-element.62, f32[4,64]{1,0:T(4,128)S(1)} %get-tuple-element.63, f32[4,3,64,8,64]{4,0,3,2,1:T(4,128)S(1)} %copy-done.10, ...), kind=kOutput, calls=%fused_computation.45 | convolution fusion | flops 21627104 | bytes 7866368 | tf_op jit(solution)/shard_map/cjukr,jl->clukr/dot_general | solution.py:45
  203.3 9.6 %reshape.273 = f32[8,1,98304]{2,1,0:T(1,128)} reshape(f32[512,2,3,4,64]{4,3,2,1,0:T(4,128)} %bitcast.314) | data formatting | bytes 6291456
  223.9 10.0 %fusion = f32[64,4,512,2,3]{2,1,0,4,3:T(4,128)S(1)} fusion(f32[6,2,3,64,1,4,512]{6,5,4,3,2,1,0:T(4,128)} %param.7, f32[64,4,512,6]{2,1,0,3:T(4,128)} %slice_bitcast_fusion), kind=kLoop, calls=%fused_computation.1 | loop fusion | flops 8650752 | bytes 25165824
  233.9 21.7 %all-to-all-done.2 = f32[8,1,98304]{2,1,0:T(1,128)} async-done(((f32[8,1,98304]{2,1,0:T(1,128)}), f32[8,1,98304]{2,1,0:T(1,128)}, u32[]{:S(2)}, u32[]{:S(2)}) %all-to-all-start.2) | async-done | bytes 3145760 | tf_op jit(solution)/shard_map/all_to_all | solution.py:66
  256.2 11.7 %reduce.6 = f32[8,98304]{1,0:T(8,128)} reduce(f32[8,1,98304]{2,1,0:T(1,128)} %all-to-all-done.2, f32[]{:T(128)} %broadcast.487), dimensions={1}, to_apply=%all_to_all.20.reduce_sub_computation | reduce | bytes 6291460 | tf_op jit(solution)/shard_map/all_to_all | solution.py:66
  267.8 9.3 %reshape.274 = f32[512,2,3,4,64]{4,3,2,1,0:T(4,128)} reshape(f32[8,98304]{1,0:T(8,128)} %reduce.6) | data formatting | bytes 6291456
  288.0 9.1 %fusion.46 = f32[512,3,4,64]{0,3,2,1:T(8,128)} fusion(f32[1,3,4,64,512]{4,3,2,1,0:T(8,128)} %copy.187), kind=kOutput, calls=%fused_computation.120 | convolution fusion | flops 2419851264 | bytes 3145728 | tf_op jit(solution)/shard_map/clus,sm->culm/dot_general | solution.py:45
  297.1 7.4 fusion.44
  308.8 9.0 %subtract_bitcast_fusion.5 = f32[1,3,64,1,4,512]{5,2,4,1,3,0:T(8,128)S(1)} fusion(f32[512,3,4,64]{0,3,2,1:T(8,128)} %fusion.46, f32[1,3,4,64,512]{4,3,2,1,0:T(8,128)} %copy.186), kind=kOutput, calls=%fused_computation.142 | convolution fusion | flops 2419982336 | bytes 4718592 | tf_op jit(solution)/shard_map/clus,sm->culm/dot_general | solution.py:45
  317.8 7.5 add_bitcast_fusion.4
  358.3 9.6 %reshape.275 = f32[8,1,98304]{2,1,0:T(1,128)} reshape(f32[512,2,3,4,64]{4,3,2,1,0:T(4,128)} %bitcast.315) | data formatting | bytes 6291456
  367.9 41.4 %all_to_all.30 = f32[8,1,98304]{2,1,0:T(1,128)S(1)} all-to-all(f32[8,1,98304]{2,1,0:T(1,128)} %reshape.275), channel_id=1, replica_groups=mesh['bx'=8,'by'=4] {'bx'}, dimensions={0} | all-to-all | bytes 6291456 | tf_op jit(solution)/shard_map/all_to_all | solution.py:66
  409.2 11.1 %reduce.7 = f32[8,98304]{1,0:T(8,128)} reduce(f32[8,1,98304]{2,1,0:T(1,128)S(1)} %all_to_all.30, f32[]{:T(128)} %broadcast.487), dimensions={1}, to_apply=%all_to_all.21.reduce_sub_computation | reduce | bytes 6291460 | tf_op jit(solution)/shard_map/all_to_all | solution.py:66
  420.3 9.3 %reshape.276 = f32[512,2,3,4,64]{4,3,2,1,0:T(4,128)} reshape(f32[8,98304]{1,0:T(8,128)} %reduce.7) | data formatting | bytes 6291456
  470.6 7.8 %add_bitcast_fusion = f32[3,4,64,8,64]{4,1,3,2,0:T(4,128)S(1)} fusion(f32[4,3,64,8,64]{4,0,3,2,1:T(4,128)} %fusion.99, f32[3,4,64,8,64]{4,1,3,2,0:T(4,128)} %copy.132, f32[3,4,64,8,64]{4,1,3,2,0:T(4,128)S(1)} %copy.131, f32[4,64]{1,0:T(4,128)S(1)} %get-tuple-element.61, f32[4,64]{1,0:T(4,128)S(1)} %get-tuple-element.63), kind=kOutput, calls=%fused_computation.39 | convolution fusion | flops 20447456 | bytes 6293504 | tf_op jit(solution)/shard_map/clukr,lj->cjukr/dot_general | solution.py:46
  494.4 14.5 %copy.105 = f32[6,4,256,512]{2,1,3,0:T(4,128)} copy(f32[6,4,256,512]{3,2,1,0:T(8,128)} %param.10) | data formatting | bytes 25165824 | tf_op args[4]
  508.9 9.6 %slice_bitcast_fusion.14 = (f32[3,256,512]{1,0,2:T(4,128)}, f32[3,256,512]{1,0,2:T(4,128)}, f32[3,256,512]{1,0,2:T(4,128)}, f32[3,256,512]{1,0,2:T(4,128)}, f32[3,256,512]{1,0,2:T(4,128)}, /*index=5*/f32[3,256,512]{1,0,2:T(4,128)}) fusion(f32[6,4,256,512]{2,1,3,0:T(4,128)} %copy.105), kind=kLoop, calls=%fused_computation.90 | loop fusion | bytes 18874368 | tf_op jit(solution)/shard_map/slice | solution.py:82
  518.6 7.6 copy.149
  540.2 21.7 %all-to-all-done.4 = f32[2,3,256,512]{3,0,1,2:T(2,128)S(1)} async-done(((f32[2,3,256,512]{3,0,1,2:T(2,128)}), f32[2,3,256,512]{3,0,1,2:T(2,128)S(1)}, u32[]{:S(2)}, u32[]{:S(2)}) %all-to-all-start.4) | async-done | bytes 3145760 | tf_op jit(solution)/shard_map/all_to_all | solution.py:62
  597.0 10.7 %maximum_bitcast_fusion.2 = (f32[4,258,514]{1,0,2:T(4,128)}, f32[4,258,514]{1,0,2:T(4,128)}) fusion(f32[6,4,258,1]{2,1,3,0:T(4,128)S(1)} %collective-permute-done.3, f32[6,4,258,1]{2,1,3,0:T(4,128)S(1)} %collective-permute-done.2, f32[6,4,1,512]{2,1,3,0:T(4,128)} %copy.106, f32[6,4,256,512]{2,1,3,0:T(4,128)} %copy.105, f32[6,4,1,512]{2,1,3,0:T(4,128)} %copy.104), kind=kLoop, calls=%fused_computation.30 | loop fusion | flops 4243584 | bytes 16974336 | tf_op jit(solution)/shard_map/squeeze | solution.py:106
  607.7 13.8 %maximum_bitcast_fusion.3 = (f32[4,258,514]{1,0,2:T(4,128)}, f32[4,258,514]{1,0,2:T(4,128)}, f32[4,258,514]{1,0,2:T(4,128)}) fusion(f32[6,4,258,1]{2,1,3,0:T(4,128)S(1)} %collective-permute-done.3, f32[6,4,258,1]{2,1,3,0:T(4,128)S(1)} %collective-permute-done.2, f32[6,4,1,512]{2,1,3,0:T(4,128)} %copy.106, f32[6,4,256,512]{2,1,3,0:T(4,128)} %copy.105, ...), kind=kLoop, calls=%fused_computation.31 | loop fusion | flops 6365376 | bytes 19096128 | tf_op jit(solution)/shard_map/squeeze | solution.py:105
  633.4 8.9 %fusion.35 = (f32[1,4,256,512]{2,1,3,0:T(4,128)S(1)}, f32[1,4,256,512]{2,1,3,0:T(4,128)S(1)}) fusion(f32[4,258,514]{1,0,2:T(4,128)S(1)} %copy-done.2, f32[4,258,514]{1,0,2:T(4,128)S(1)} %copy-done.8, f32[3,256,512]{1,0,2:T(4,128)} %get-tuple-element.30, f32[1,256,512]{1,0,2:T(1,128)S(1)} %get-tuple-element.55, f32[3,256,512]{1,0,2:T(4,128)S(1)} %copy-done.16, ...), kind=kLoop, calls=%fused_computation.95 | loop fusion | flops 7340032 | bytes 28311552 | tf_op jit(solution)/shard_map/stack | solution.py:103
  676.4 7.7 %copy.161 = f32[3,4,256,512]{3,2,1,0:T(8,128)} copy(f32[3,4,256,512]{2,1,3,0:T(4,128)} %copy-done) | data formatting | bytes 12582912
  684.1 22.9 %fusion.2 = (f32[3,4,256,512]{2,1,3,0:T(4,128)S(1)}, f32[3,4,256,512]{2,1,3,0:T(4,128)S(1)}) fusion(f32[3,4,258,1]{2,1,3,0:T(4,128)S(1)} %collective-permute-done.7, f32[3,4,1,512]{2,1,3,0:T(4,128)S(1)} %copy-done.3, f32[3,4,256,512]{2,1,3,0:T(4,128)} %copy-done, f32[3,4,1,512]{2,1,3,0:T(4,128)} %copy.153, f32[3,4,258,1]{2,1,3,0:T(4,128)S(1)} %collective-permute-done.6), kind=kLoop, calls=%fused_computation.7 | loop fusion | flops 18874368 | bytes 18948288 | tf_op jit(solution)/shard_map/mul | solution.py:78
  723.2 8.0 %multiply_add_fusion = f32[6,4,256,512]{2,1,3,0:T(4,128)S(1)} fusion(f32[6,4,256,512]{2,1,3,0:T(4,128)S(1)} %bitcast.307, f32[6,4,256,512]{2,1,3,0:T(4,128)} %fusion.19), kind=kLoop, calls=%fused_computation.3 | loop fusion | flops 6291456 | bytes 37748736 | tf_op jit(solution)/shard_map/add | solution.py:137
  750.9 14.5 %copy.162 = f32[6,4,256,512]{3,2,1,0:T(8,128)} copy(f32[6,4,256,512]{2,1,3,0:T(4,128)} %pad_maximum_fusion) | data formatting | bytes 25165824
  (204 shorter events, 311.6 us)
Async XLA Ops:
  3.4 31.8 %all-to-all-start = ((f32[3,256,512]{1,0,2:T(4,128)}), f32[3,256,512]{1,0,2:T(4,128)S(1)}, u32[]{:S(2)}, u32[]{:S(2)}) async-start(f32[3,256,512]{1,0,2:T(4,128)} %copy.108), calls=%async_computation | async-start | bytes 4194304 | tf_op jit(solution)/shard_map/all_to_all | solution.py:58
  8.7 29.1 %copy-start.28 = (f32[256,8]{0,1:T(8,128)}, f32[256,8]{0,1:T(8,128)S(1)}, u32[]{:S(2)}) copy-start(f32[256,8]{0,1:T(8,128)S(1)} %get-tuple-element.65) | copy-start | bytes 24580
  67.3 73.0 %all-to-all-start.1 = ((f32[2,3,256,512]{3,0,1,2:T(2,128)}), f32[2,3,256,512]{3,0,1,2:T(2,128)S(1)}, u32[]{:S(2)}, u32[]{:S(2)}) async-start(f32[2,3,256,512]{3,0,1,2:T(2,128)} %pad_maximum_fusion.13), calls=%async_computation.1 | async-start | bytes 6291456 | tf_op jit(solution)/shard_map/all_to_all | solution.py:62
  172.9 8.1 %copy-start.10 = (f32[4,3,64,8,64]{4,0,3,2,1:T(4,128)S(1)}, f32[4,3,64,8,64]{4,0,3,2,1:T(4,128)}, u32[]{:S(2)}) copy-start(f32[4,3,64,8,64]{4,0,3,2,1:T(4,128)} %fusion.10) | copy-start | bytes 4718596
  212.9 42.7 %all-to-all-start.2 = ((f32[8,1,98304]{2,1,0:T(1,128)}), f32[8,1,98304]{2,1,0:T(1,128)}, u32[]{:S(2)}, u32[]{:S(2)}) async-start(f32[8,1,98304]{2,1,0:T(1,128)} %reshape.273), calls=%async_computation.2 | async-start | bytes 6291456 | tf_op jit(solution)/shard_map/all_to_all | solution.py:66
  288.0 9.1 %copy-start.27 = (f32[1,3,4,64,512]{4,3,2,1,0:T(8,128)S(1)}, f32[1,3,4,64,512]{4,3,2,1,0:T(8,128)}, u32[]{:S(2)}) copy-start(f32[1,3,4,64,512]{4,3,2,1,0:T(8,128)} %copy.187) | copy-start | bytes 4718596
  308.8 9.0 %copy-start.26 = (f32[1,3,4,64,512]{4,3,2,1,0:T(8,128)S(1)}, f32[1,3,4,64,512]{4,3,2,1,0:T(8,128)}, u32[]{:S(2)}) copy-start(f32[1,3,4,64,512]{4,3,2,1,0:T(8,128)} %copy.186) | copy-start | bytes 4718596
  308.8 9.0 %copy-start.30 = (f32[512,3,4,64]{0,3,2,1:T(8,128)S(1)}, f32[512,3,4,64]{0,3,2,1:T(8,128)}, u32[]{:S(2)}) copy-start(f32[512,3,4,64]{0,3,2,1:T(8,128)} %fusion.44) | copy-start | bytes 4718596
  317.8 7.5 copy-start.24
  444.6 7.3 copy-start.1
  486.7 75.2 %all-to-all-start.4 = ((f32[2,3,256,512]{3,0,1,2:T(2,128)}), f32[2,3,256,512]{3,0,1,2:T(2,128)S(1)}, u32[]{:S(2)}, u32[]{:S(2)}) async-start(f32[2,3,256,512]{3,0,1,2:T(2,128)} %copy.137), calls=%async_computation.4 | async-start | bytes 6291456 | tf_op jit(solution)/shard_map/all_to_all | solution.py:62
  491.6 34.5 %collective-permute-start = (f32[6,4,1,512]{3,1,2,0:T(4,128)S(1)}, f32[6,4,1,512]{3,1,2,0:T(4,128)S(1)}, u32[]{:S(2)}, u32[]{:S(2)}) collective-permute-start(f32[6,4,1,512]{3,1,2,0:T(4,128)S(1)} %copy.184), channel_id=1, source_target_pairs={{0,4},{4,8},{8,12},{12,16},{16,20},{20,24},{24,28},{28,0},{1,5},{5... | collective-permute-start | bytes 147464 | tf_op jit(solution)/shard_map/ppermute | solution.py:20
  491.7 39.0 %collective-permute-start.1 = (f32[6,4,1,512]{3,1,2,0:T(4,128)S(1)}, f32[6,4,1,512]{3,1,2,0:T(4,128)S(1)}, u32[]{:S(2)}, u32[]{:S(2)}) collective-permute-start(f32[6,4,1,512]{3,1,2,0:T(4,128)S(1)} %copy.185), channel_id=1, source_target_pairs={{4,0},{8,4},{12,8},{16,12},{20,16},{24,20},{28,24},{0,28},{5,1},{9... | collective-permute-start | bytes 147464 | tf_op jit(solution)/shard_map/ppermute | solution.py:23
  536.1 60.9 %collective-permute-start.2 = (f32[6,4,258,1]{2,1,3,0:T(4,128)S(1)}, f32[6,4,258,1]{2,1,3,0:T(4,128)S(1)}, u32[]{:S(2)}, u32[]{:S(2)}) collective-permute-start(f32[6,4,258,1]{2,1,3,0:T(4,128)S(1)} %get-tuple-element.17), channel_id=1, source_target_pairs={{0,1},{1,2},{2,3},{3,0},{4,5},{5,6},{6,7},{7,4},{8,9},{9,10},{10,1... | collective-permute-start | bytes 74312 | tf_op jit(solution)/shard_map/ppermute | solution.py:20
  538.1 58.8 %collective-permute-start.3 = (f32[6,4,258,1]{2,1,3,0:T(4,128)S(1)}, f32[6,4,258,1]{2,1,3,0:T(4,128)S(1)}, u32[]{:S(2)}, u32[]{:S(2)}) collective-permute-start(f32[6,4,258,1]{2,1,3,0:T(4,128)S(1)} %get-tuple-element.18), channel_id=1, source_target_pairs={{1,0},{2,1},{3,2},{0,3},{5,4},{6,5},{7,6},{4,7},{9,8},{10,9},{11,1... | collective-permute-start | bytes 74312 | tf_op jit(solution)/shard_map/ppermute | solution.py:23
  592.3 15.4 %slice-start.5 = ((s8[6291456]{0:T(1024)(128)(4,1)}), s8[2097152]{0:T(1024)(128)(4,1)S(1)}, s32[]{:S(2)}) async-start(s8[6291456]{0:T(1024)(128)(4,1)} %bitcast.310), calls=%async_computation.11 | async-start | bytes 4194304
  592.3 31.3 %all-to-all-start.5 = ((f32[3,256,512]{1,0,2:T(4,128)}), f32[3,256,512]{1,0,2:T(4,128)}, u32[]{:S(2)}, u32[]{:S(2)}) async-start(f32[3,256,512]{1,0,2:T(4,128)} %copy.143), calls=%async_computation.5 | async-start | bytes 4194304 | tf_op jit(solution)/shard_map/all_to_all | solution.py:58
  596.9 10.7 %slice-start.6 = ((s8[6291456]{0:T(1024)(128)(4,1)}), s8[4194304]{0:T(1024)(128)(4,1)S(1)}, s32[]{:S(2)}) async-start(s8[6291456]{0:T(1024)(128)(4,1)} %bitcast.310), calls=%async_computation.12 | async-start | bytes 8388608
  625.8 6.7 copy-start.18
  627.1 6.3 copy-start.17
  632.5 9.8 %slice-start.7 = ((s8[6291456]{0:T(1024)(128)(4,1)}), s8[4194304]{0:T(1024)(128)(4,1)S(1)}, s32[]{:S(2)}) async-start(s8[6291456]{0:T(1024)(128)(4,1)} %bitcast.316), calls=%async_computation.13 | async-start | bytes 8388608
  633.4 8.9 %slice-start.8 = ((s8[6291456]{0:T(1024)(128)(4,1)}), s8[2097152]{0:T(1024)(128)(4,1)S(1)}, s32[]{:S(2)}) async-start(s8[6291456]{0:T(1024)(128)(4,1)} %bitcast.316), calls=%async_computation.14 | async-start | bytes 4194304
  651.9 10.1 %collective-permute-start.4 = (f32[3,4,1,512]{3,1,2,0:T(4,128)S(1)}, f32[3,4,1,512]{3,1,2,0:T(4,128)S(1)}, u32[]{:S(2)}, u32[]{:S(2)}) collective-permute-start(f32[3,4,1,512]{3,1,2,0:T(4,128)S(1)} %copy.150), channel_id=1, source_target_pairs={{4,0},{8,4},{12,8},{16,12},{20,16},{24,20},{28,24},{0,28},{5,1},{9... | collective-permute-start | bytes 73736 | tf_op jit(solution)/shard_map/ppermute | solution.py:23
  653.6 11.2 %collective-permute-start.5 = (f32[3,4,1,512]{3,1,2,0:T(4,128)S(1)}, f32[3,4,1,512]{3,1,2,0:T(4,128)S(1)}, u32[]{:S(2)}, u32[]{:S(2)}) collective-permute-start(f32[3,4,1,512]{3,1,2,0:T(4,128)S(1)} %copy.152), channel_id=1, source_target_pairs={{0,4},{4,8},{8,12},{12,16},{16,20},{20,24},{24,28},{28,0},{1,5},{5... | collective-permute-start | bytes 73736 | tf_op jit(solution)/shard_map/ppermute | solution.py:20
  668.6 15.5 %collective-permute-start.6 = (f32[3,4,258,1]{2,1,3,0:T(4,128)S(1)}, f32[3,4,258,1]{2,1,3,0:T(4,128)S(1)}, u32[]{:S(2)}, u32[]{:S(2)}) collective-permute-start(f32[3,4,258,1]{2,1,3,0:T(4,128)S(1)} %get-tuple-element.23), channel_id=1, source_target_pairs={{1,0},{2,1},{3,2},{0,3},{5,4},{6,5},{7,6},{4,7},{9,8},{10,9},{11,1... | collective-permute-start | bytes 37160 | tf_op jit(solution)/shard_map/ppermute | solution.py:23
  670.1 14.0 %collective-permute-start.7 = (f32[3,4,258,1]{2,1,3,0:T(4,128)S(1)}, f32[3,4,258,1]{2,1,3,0:T(4,128)S(1)}, u32[]{:S(2)}, u32[]{:S(2)}) collective-permute-start(f32[3,4,258,1]{2,1,3,0:T(4,128)S(1)} %get-tuple-element.24), channel_id=1, source_target_pairs={{0,1},{1,2},{2,3},{3,0},{4,5},{5,6},{6,7},{7,4},{8,9},{9,10},{10,1... | collective-permute-start | bytes 37160 | tf_op jit(solution)/shard_map/ppermute | solution.py:20
  676.4 7.7 %copy-start.3 = (f32[3,4,1,512]{2,1,3,0:T(4,128)S(1)}, f32[3,4,1,512]{2,1,3,0:T(4,128)}, u32[]{:S(2)}) copy-start(f32[3,4,1,512]{2,1,3,0:T(4,128)} %copy.151) | copy-start | bytes 73732
  684.1 22.9 %copy-start.4 = (f32[3,256,512]{1,0,2:T(4,128)S(1)}, f32[3,256,512]{1,0,2:T(4,128)}, u32[]{:S(2)}) copy-start(f32[3,256,512]{1,0,2:T(4,128)} %get-tuple-element.41) | copy-start | bytes 4718596
  684.1 22.9 %copy-start.5 = (f32[3,256,512]{1,0,2:T(4,128)S(1)}, f32[3,256,512]{1,0,2:T(4,128)}, u32[]{:S(2)}) copy-start(f32[3,256,512]{1,0,2:T(4,128)} %get-tuple-element.42) | copy-start | bytes 4718596
  684.1 22.9 %copy-start.21 = (f32[1,256,512]{1,0,2:T(1,128)S(1)}, f32[1,256,512]{1,0,2:T(1,128)}, u32[]{:S(2)}) copy-start(f32[1,256,512]{1,0,2:T(1,128)} %copy.156) | copy-start | bytes 1572868
  714.7 8.5 %slice-start = ((s8[12582912]{0:T(1024)(128)(4,1)}), s8[4194304]{0:T(1024)(128)(4,1)S(1)}, s32[]{:S(2)}) async-start(s8[12582912]{0:T(1024)(128)(4,1)} %bitcast.306), calls=%async_computation.6 | async-start | bytes 8388608
  716.7 6.6 slice-start.1
  (21 other events, 83.0 us)
where the time goes:
time: 777 us; the launch traced here: 766 us
  local copies, waits for them, and re-layouts  240 us (31%)
  other arithmetic  160 us (21%)
  matrix products  150 us (19%)
  waiting for transfers between devices  140 us (18%)
  blocking collectives  41.4 us (5%)
  starting transfers between devices  32.9 us (4%)
    unnamed x95, local copies, waits for them, and re-layouts  102 us
    all_to_all x2, waiting for transfers between devices, dip_blocks(): return lax.all_to_all(block, 'by', split_axis=2, concat_axis=2, tiled=True)  89.5 us
    all_to_all x1, blocking collectives, strike_modes(): return lax.all_to_all(block, 'bx', split_axis=4, concat_axis=4, tiled=True)  41.4 us
    dot_general x4, matrix products, complex_apply(): contract(real_part, table[0]) - contract(imag_part, table[1])  32.4 us
    dot_general x4, matrix products, complex_apply(): contract(imag_part, table[0])  29.5 us
    dot_general x4, matrix products, complex_apply(): contract(real_part, table[1]) + contract(imag_part, table[0])  29.4 us
    dot_general x4, matrix products, complex_apply(): contract(imag_part, table[1])  29.2 us
    all_to_all x2, waiting for transfers between devices, plane_blocks(): return lax.all_to_all(block, 'bx', split_axis=2, concat_axis=2, tiled=True)  28.6 us
  transfers between devices with their start and end apart: 13, of which 5 were waited for; matrix products, arithmetic and copies ran while one was open for 18% of the time, Pallas kernels for 0%

commit v1 on v0

v1 whole, which is shorter than its diff:
```python
from functools import partial
import math

import jax
import jax.numpy as jnp
import numpy as np
from jax import lax
from jax.experimental import pallas as pl
from jax.experimental.pallas import tpu as pltpu
from jax.sharding import PartitionSpec as P

COURANT = 0.3
FRICTION = 0.6
CHUNKS = 1
F32 = jnp.float32
BF16 = jnp.bfloat16


def halves(table):
    high = np.asarray(table, np.float32).astype(BF16)
    low = (np.asarray(table, np.float64) - high.astype(np.float64)).astype(BF16)
    return np.stack([high, low])


def square_table(length):
    index = np.arange(length)
    angle = 2.0 * math.pi / length * (index[:, None] * index[None, :] % length)
    return jnp.asarray(np.stack([halves(np.cos(angle)), halves(np.sin(angle))]))


def split(value):
    high = value.astype(BF16)
    return high, (value - high.astype(F32)).astype(BF16)


def product(value, table, left):
    def dot(a, b):
        if left:
            a, b = b, a
        return lax.dot_general(a, b, (((1,), (0,)), ((), ())), preferred_element_type=F32)

    return dot(value[0], table[0]) + (dot(value[0], table[1]) + dot(value[1], table[0]))


def complex_product(real_part, imag_part, table_ref, sign, left):
    cos = (table_ref[0, 0], table_ref[0, 1])
    sin = (table_ref[1, 0], table_ref[1, 1])
    real_part, imag_part = split(real_part), split(imag_part)
    return (
        product(real_part, cos, left) - sign * product(imag_part, sin, left),
        product(imag_part, cos, left) + sign * product(real_part, sin, left),
    )


def root(index, count):
    angle = 2.0 * math.pi * (index % count) / count
    cos, sin = math.cos(angle), math.sin(angle)
    return [float(round(v)) if abs(v - round(v)) < 1e-12 else v for v in (cos, sin)]


def add_term(total, factor, value):
    if factor == 0.0:
        return total
    term = value if factor == 1.0 else (-value if factor == -1.0 else factor * value)
    return term if total is None else total + term


def strike_forward(count, x_ref, o_ref):
    for c in range(x_ref.shape[1]):
        for r in range(count):
            real_part = imag_part = None
            for b in range(count):
                cos, sin = root(r * b, count)
                real_part = add_term(real_part, cos, x_ref[b, c])
                imag_part = add_term(imag_part, -sin, x_ref[b, c])
            o_ref[r, 0, c] = real_part
            o_ref[r, 1, c] = jnp.zeros_like(real_part) if imag_part is None else imag_part


def strike_inverse(count, scale, x_ref, o_ref):
    for c in range(x_ref.shape[2]):
        for b in range(count):
            total = None
            for r in range(count):
                cos, sin = root(r * b, count)
                total = add_term(total, cos, x_ref[r, 0, c])
                total = add_term(total, -sin, x_ref[r, 1, c])
            o_ref[b, c] = scale * total


def strike_cells_dft(sign, x_ref, tw_ref, table_ref, o_ref, held):
    blocks, _, _, rows, _ = x_ref.shape
    for s in range(blocks):
        for z in range(2):
            held[z, pl.ds(s * rows, rows), :] = x_ref[s, z, 0]
    cos, sin = tw_ref[:, 0:1], sign * tw_ref[:, 1:2]
    real_part, imag_part = held[0], held[1]
    if sign < 0:
        real_part, imag_part = (
            real_part * cos - imag_part * sin,
            real_part * sin + imag_part * cos,
        )
    real_part, imag_part = complex_product(real_part, imag_part, table_ref, sign, True)
    if sign > 0:
        real_part, imag_part = (
            real_part * cos - imag_part * sin,
            real_part * sin + imag_part * cos,
        )
    held[0] = real_part
    held[1] = imag_part
    blocks, _, _, rows, _ = o_ref.shape
    for s in range(blocks):
        for z in range(2):
            o_ref[s, z, 0] = held[z, pl.ds(s * rows, rows), :]


def dip_response(scale, x_ref, tw_ref, table_ref, now_ref, past_ref, o_ref, held):
    count, _, _, rows, _ = x_ref.shape
    for l in range(count):
        real_part = imag_part = None
        for j in range(count):
            cos, sin = root(l * j, count)
            real_part = add_term(real_part, cos, x_ref[j, 0, 0])
            real_part = add_term(real_part, sin, x_ref[j, 1, 0])
            imag_part = add_term(imag_part, cos, x_ref[j, 1, 0])
            imag_part = add_term(imag_part, -sin, x_ref[j, 0, 0])
        cos, sin = tw_ref[0, l : l + 1, :], tw_ref[1, l : l + 1, :]
        held[0, pl.ds(l * rows, rows), :] = real_part * cos + imag_part * sin
        held[1, pl.ds(l * rows, rows), :] = imag_part * cos - real_part * sin
    real_part, imag_part = complex_product(held[0], held[1], table_ref, -1.0, False)
    weight = scale * now_ref[...]
    real_part = weight * real_part + past_ref[0, 0]
    imag_part = weight * imag_part + past_ref[1, 0]
    real_part, imag_part = complex_product(real_part, imag_part, table_ref, 1.0, False)
    held[0] = real_part
    held[1] = imag_part
    for l in range(count):
        cos, sin = tw_ref[0, l : l + 1, :], tw_ref[1, l : l + 1, :]
        real_part = held[0, pl.ds(l * rows, rows), :]
        imag_part = held[1, pl.ds(l * rows, rows), :]
        held[0, pl.ds(l * rows, rows), :] = real_part * cos - imag_part * sin
        held[1, pl.ds(l * rows, rows), :] = imag_part * cos + real_part * sin
    for j in range(count):
        real_part = imag_part = None
        for l in range(count):
            cos, sin = root(l * j, count)
            lr = held[0, pl.ds(l * rows, rows), :]
            li = held[1, pl.ds(l * rows, rows), :]
            real_part = add_term(real_part, cos, lr)
            real_part = add_term(real_part, -sin, li)
            imag_part = add_term(imag_part, cos, li)
            imag_part = add_term(imag_part, sin, lr)
        o_ref[j, 0, 0] = real_part
        o_ref[j, 1, 0] = imag_part


def rows_diff(value, before, after):
    count = value.shape[0]
    row = lax.broadcasted_iota(jnp.int32, value.shape, 0)
    low = jnp.where(row == 0, before, pltpu.roll(value, 1, 0))
    high = jnp.where(row == count - 1, after, pltpu.roll(value, count - 1, 0))
    return 0.5 * (high - low)


def cols_diff(value, before, after):
    count = value.shape[1]
    col = lax.broadcasted_iota(jnp.int32, value.shape, 1)
    low = jnp.where(col == 0, before, pltpu.roll(value, 1, 1))
    high = jnp.where(col == count - 1, after, pltpu.roll(value, count - 1, 1))
    return 0.5 * (high - low)


def layer_diff(layers, ghost, z):
    low = ghost if z == 0 else layers(z - 1)
    return 0.5 * (layers(z + 1) - low)


def strike_edges(low_ref, prev_ref, high_ref, next_ref, slot, component, z):
    i, last = pl.program_id(0), pl.num_programs(0) - 1
    before = jnp.where(i == 0, low_ref[slot, z : z + 1, :], prev_ref[component, z, 7:8, :])
    after = jnp.where(i == last, high_ref[slot, z : z + 1, :], next_ref[component, z, 0:1, :])
    return before, after


def velocity_step(s_ref, prev_ref, next_ref, low_ref, high_ref, col_ref, v_ref, t_ref, o_ref, c_ref):
    layers = v_ref.shape[1]
    width = v_ref.shape[3]
    half = 3 * layers
    for component, (sx, sy, sz) in enumerate(((0, 3, 4), (3, 1, 5), (4, 5, 2))):
        for z in range(layers):
            before, after = strike_edges(low_ref, prev_ref, high_ref, next_ref, component, sx, z)
            total = rows_diff(s_ref[sx, z], before, after)
            k = component * layers + z
            total = total + cols_diff(
                s_ref[sy, z], col_ref[:, k : k + 1], col_ref[:, half + k : half + k + 1]
            )
            low = t_ref[component] if z == 0 else s_ref[sz, z - 1]
            if z + 1 < layers:
                total = total + 0.5 * (s_ref[sz, z + 1] - low)
            else:
                total = total - 0.5 * low
            value = v_ref[component, z] + COURANT * total
            o_ref[component, z] = value
            c_ref[:, k : k + 1] = value[:, 0:1]
            c_ref[:, half + k : half + k + 1] = value[:, width - 1 : width]


def stress_step(v_ref, prev_ref, next_ref, low_ref, high_ref, col_ref, w_ref, s_ref, y_ref, o_ref):
    layers = v_ref.shape[1]
    half = 3 * layers
    for z in range(layers):
        dx, dy, dz = [], [], []
        for c in range(3):
            before, after = strike_edges(low_ref, prev_ref, high_ref, next_ref, c, c, z)
            k = c * layers + z
            dx.append(rows_diff(v_ref[c, z], before, after))
            dy.append(
                cols_diff(v_ref[c, z], col_ref[:, k : k + 1], col_ref[:, half + k : half + k + 1])
            )
            low = w_ref[c] if z == 0 else v_ref[c, z - 1]
            if z + 1 < layers:
                dz.append(0.5 * (v_ref[c, z + 1] - low))
            else:
                dz.append(-0.5 * low)
        dilation = dx[0] + dy[1] + dz[2]
        xx = s_ref[0, z] + COURANT * (dilation + 2.0 * dx[0])
        yy = s_ref[1, z] + COURANT * (dilation + 2.0 * dy[1])
        zz = s_ref[2, z] + COURANT * (dilation + 2.0 * dz[2])
        xy = s_ref[3, z] + COURANT * (dy[0] + dx[1])
        xz = s_ref[4, z] + COURANT * (dz[0] + dx[2])
        yz = s_ref[5, z] + COURANT * (dz[1] + dy[2])
        pressure = (xx + yy + zz) / 3.0
        xx, yy, zz = xx - pressure, yy - pressure, zz - pressure
        shear = jnp.sqrt(0.5 * (xx * xx + yy * yy + zz * zz) + (xy * xy + xz * xz + yz * yz))
        limit = y_ref[z] + FRICTION * jnp.maximum(-pressure, 0.0)
        factor = limit / jnp.maximum(shear, limit)
        o_ref[0, z] = pressure + factor * xx
        o_ref[1, z] = pressure + factor * yy
        o_ref[2, z] = pressure + factor * zz
        o_ref[3, z] = factor * xy
        o_ref[4, z] = factor * xz
        o_ref[5, z] = factor * yz


def whole_block(shape):
    return pl.BlockSpec(shape, lambda *_: (0,) * len(shape))


def component_block(shape, dim):
    block = tuple(1 if d == dim else n for d, n in enumerate(shape))
    return pl.BlockSpec(block, lambda c: tuple(c if d == dim else 0 for d in range(len(shape))))


def struct(shape):
    return jax.ShapeDtypeStruct(shape, F32)


def cost(flops, *arrays):
    moved = sum(math.prod(a.shape) * a.dtype.itemsize for a in arrays)
    return pl.CostEstimate(flops=int(flops), bytes_accessed=int(moved), transcendentals=0)


def ring(axis):
    count = lax.axis_size(axis)
    forward = [(i, (i + 1) % count) for i in range(count)]
    return forward, [(b, a) for a, b in forward]


def exchange(block, axis):
    return lax.all_to_all(block, axis, split_axis=0, concat_axis=0)


def edges(first, last, axis):
    forward, backward = ring(axis)
    return lax.ppermute(last, axis, forward), lax.ppermute(first, axis, backward)


def fault_traction(interface, now, past, tables, scale):
    strike_count, dip_count = lax.axis_size("bx"), lax.axis_size("by")
    count, cells, width = interface.shape
    rows, modes = cells // strike_count, cells // dip_count
    strike_tw, strike_table, dip_tw, dip_table = tables
    block = interface.reshape(count, strike_count, rows, width).transpose(1, 0, 2, 3)
    block = exchange(block, "bx")
    wide = struct((strike_count, 2, count, rows, width))
    tall = struct((dip_count, 2, count, modes, width))
    block = pl.pallas_call(
        partial(strike_forward, strike_count),
        out_shape=wide,
        cost_estimate=cost(wide.size * 2 * strike_count, block, wide),
        name="strike_forward",
    )(block)
    block = exchange(block, "bx")

    def cells_dft(block, sign, out):
        return pl.pallas_call(
            partial(strike_cells_dft, sign),
            grid=(count,),
            in_specs=[
                component_block(block.shape, 2),
                whole_block(strike_tw.shape),
                whole_block(strike_table.shape),
            ],
            out_specs=component_block(out.shape, 2),
            out_shape=out,
            scratch_shapes=[pltpu.VMEM((2, cells, width), F32)],
            cost_estimate=cost(24 * count * cells * cells * width, block, out),
            name="strike_cells",
        )(block, strike_tw, strike_table)

    block = exchange(cells_dft(block, -1.0, tall), "by")
    block = pl.pallas_call(
        partial(dip_response, scale),
        grid=(count,),
        in_specs=[
            component_block(block.shape, 2),
            whole_block(dip_tw.shape),
            whole_block(dip_table.shape),
            whole_block(now.shape),
            component_block(past.shape, 1),
        ],
        out_specs=component_block(tall.shape, 2),
        out_shape=tall,
        scratch_shapes=[pltpu.VMEM((2, cells, width), F32)],
        cost_estimate=cost(48 * count * cells * width * width, block, tall, past, now),
        name="dip_response",
    )(block, dip_tw, dip_table, now, past)
    block = exchange(block, "by")
    block = exchange(cells_dft(block, 1.0, wide), "bx")
    flat = struct((strike_count, count, rows, width))
    block = pl.pallas_call(
        partial(strike_inverse, strike_count, scale),
        out_shape=flat,
        cost_estimate=cost(wide.size * 2 * strike_count, block, flat),
        name="strike_inverse",
    )(block)
    block = exchange(block, "bx")
    return block.transpose(1, 0, 2, 3).reshape(count, cells, width)


def tile_spec(shape, tile):
    block = shape[:-2] + (tile, shape[-1])
    lead = (0,) * (len(shape) - 2)
    return pl.BlockSpec(block, lambda i: lead + (i, 0))


def halo_specs(shape, tile):
    block = shape[:-2] + (8, shape[-1])
    lead = (0,) * (len(shape) - 2)
    step, last = tile // 8, shape[-2] // 8 - 1
    return [
        pl.BlockSpec(block, lambda i: lead + (jnp.maximum(i * step - 1, 0), 0)),
        pl.BlockSpec(block, lambda i: lead + (jnp.minimum((i + 1) * step, last), 0)),
    ]


def local(interface_velocity, history, kernel, velocity, stress, cohesion):
    strike_count, dip_count = lax.axis_size("bx"), lax.axis_size("by")
    _, layers, cells, width = velocity.shape
    strike_length, dip_length = cells * strike_count, width * dip_count
    scale = 1.0 / math.sqrt(strike_length * dip_length)
    angle = (2.0 * math.pi / strike_length) * (
        jnp.arange(cells, dtype=jnp.int32) * lax.axis_index("bx")
    ).astype(F32)
    strike_tw = jnp.stack([jnp.cos(angle), jnp.sin(angle)], axis=1)
    lane = np.outer(np.arange(dip_count), np.arange(width)) * (2.0 * math.pi / dip_length)
    dip_tw = jnp.asarray(np.stack([np.cos(lane), np.sin(lane)]).astype(np.float32))
    tables = (strike_tw, square_table(cells), dip_tw, square_table(width))

    past = kernel[1] * history[0]
    for h in range(1, history.shape[0]):
        past = past + kernel[h + 1] * history[h]
    modes = history.shape[3]
    past = past.reshape(2, 3, modes, dip_count, width).transpose(0, 1, 3, 2, 4)
    past = past.reshape(2, 3, cells, width)
    now = kernel[0].reshape(modes, dip_count, width).transpose(1, 0, 2).reshape(cells, width)

    step = 3 // CHUNKS
    traction = jnp.concatenate(
        [
            fault_traction(
                interface_velocity[c : c + step], now, past[:, c : c + step], tables, scale
            )
            for c in range(0, 3, step)
        ],
        axis=0,
    )

    tile = min(32, cells)
    grid = (cells // tile,)
    col_shape = (cells, 6 * layers)

    def columns(first, last):
        low, high = edges(first, last, "by")
        return jnp.concatenate([low, high], axis=1)

    def side(position):
        flat = [stress[c, :, :, position] for c in (3, 1, 5)]
        return jnp.concatenate(flat, axis=0).T

    def line(position):
        return jnp.stack([stress[c, :, position, :] for c in (0, 3, 4)])

    cols = columns(side(0), side(width - 1))
    low, high = edges(line(0), line(cells - 1), "bx")
    velocity_new, new_cols = pl.pallas_call(
        velocity_step,
        grid=grid,
        in_specs=[
            tile_spec(stress.shape, tile),
            *halo_specs(stress.shape, tile),
            whole_block(low.shape),
            whole_block(high.shape),
            tile_spec(col_shape, tile),
            tile_spec(velocity.shape, tile),
            tile_spec(traction.shape, tile),
        ],
        out_specs=[tile_spec(velocity.shape, tile), tile_spec(col_shape, tile)],
        out_shape=[struct(velocity.shape), struct(col_shape)],
        cost_estimate=cost(1e7, stress, velocity, velocity),
        name="velocity_step",
    )(stress, stress, stress, low, high, cols, velocity, traction)
    half = 3 * layers
    cols = columns(new_cols[:, :half], new_cols[:, half:])
    low, high = edges(velocity_new[:, :, 0], velocity_new[:, :, cells - 1], "bx")
    stress_new = pl.pallas_call(
        stress_step,
        grid=grid,
        in_specs=[
            tile_spec(velocity.shape, tile),
            *halo_specs(velocity.shape, tile),
            whole_block(low.shape),
            whole_block(high.shape),
            tile_spec(col_shape, tile),
            tile_spec(interface_velocity.shape, tile),
            tile_spec(stress.shape, tile),
            tile_spec(cohesion.shape, tile),
        ],
        out_specs=tile_spec(stress.shape, tile),
        out_shape=struct(stress.shape),
        cost_estimate=cost(2e7, stress, stress, velocity),
        name="stress_step",
    )(velocity_new, velocity_new, velocity_new, low, high, cols, interface_velocity, stress, cohesion)
    return velocity_new, stress_new


def solution(mesh):
    return jax.shard_map(
        local,
        mesh=mesh,
        in_specs=(
            P(None, "bx", "by"),
            P(None, None, None, "by", "bx", None, None),
            P(None, "by", "bx", None, None),
            P(None, None, "bx", "by"),
            P(None, None, "bx", "by"),
            P(None, "bx", "by"),
        ),
        out_specs=(P(None, None, "bx", "by"), P(None, None, "bx", "by")),
        check_vma=False,
    )
```

time: 777 us -> 378 us (0.49); the launches traced: 766 us -> 377 us
  local copies, waits for them, and re-layouts: 240 us -> 32 us
  other arithmetic: 160 us -> 8.81 us
  matrix products: 150 us -> 0 us
  blocking collectives: 41.4 us -> 144 us
  Pallas kernels: 0 us -> 69.6 us
  waiting for transfers between devices: 140 us -> 100 us
  starting transfers between devices: 32.9 us -> 21 us
    dot_general x20 -> x0, matrix products: 130 us -> none  [the longest x4 32.4 us: complex_apply(): contract(real_part, table[0]) - contract(imag_part, table[1])]
    all_to_all x1 -> x3, blocking collectives: 41.4 us -> 144 us  [exchange(): return lax.all_to_all(block, axis, split_axis=0, concat_axis=0)]
    unnamed x95 -> x20, local copies, waits for them, and re-layouts: 102 us -> 8.79 us
    pallas_call x0 -> x7, Pallas kernels: none -> 69.6 us  [the longest x1 17.4 us: local(): pl.pallas_call(stress_step, grid=grid, in_specs=[tile_spec(velocity.shape...]
    slice x17 -> x3, local copies, waits for them, and re-layouts: 67.9 us -> 5.57 us  [the longest x1 3.45 us: side(): flat = [stress[c, :, :, position] for c in (3, 1, 5)]]
    all_to_all x5 -> x3, waiting for transfers between devices: 140 us -> 94.2 us  [exchange(): return lax.all_to_all(block, axis, split_axis=0, concat_axis=0)]
    another operation x9 -> x3, local copies, waits for them, and re-layouts: 30.3 us -> 0.81 us  [the longest x1 0.79 us: local(): strike_tw = jnp.stack([jnp.cos(angle), jnp.sin(angle)], axis=1)]
    another operation x7 -> x3, other arithmetic: 26.5 us -> 0.02 us  [the longest x2 0.02 us: line(): return jnp.stack([stress[c, :, position, :] for c in (0, 3, 4)])]
  transfers between devices with their start and end apart: 13 -> 11, of which waited for: 5 -> 6; matrix products, arithmetic and copies ran while one was open for 18% -> 9% of each run, Pallas kernels for 0% -> 0%
where the time goes in v1:
time: 378 us; the launch traced here: 377 us
  blocking collectives  144 us (38%)
  waiting for transfers between devices  100 us (26%)
  Pallas kernels  69.6 us (18%)
  local copies, waits for them, and re-layouts  32 us (8%)
  starting transfers between devices  21 us (6%)
  other arithmetic  8.81 us (2%)
    all_to_all x3, blocking collectives, exchange(): return lax.all_to_all(block, axis, split_axis=0, concat_axis=0)  144 us
    all_to_all x3, waiting for transfers between devices, exchange(): return lax.all_to_all(block, axis, split_axis=0, concat_axis=0)  94.2 us
    pallas_call x1, Pallas kernels, local(): pl.pallas_call(stress_step, grid=grid, in_specs=[tile_spec(velocity.shape...  17.4 us
    pallas_call x1, Pallas kernels, local(): pl.pallas_call(velocity_step, grid=grid, in_specs=[tile_spec(stress.shape...  17 us
    pallas_call x1, Pallas kernels, fault_traction(): pl.pallas_call(partial(dip_response, scale), grid=(count,), in_specs=[com...  14.9 us
    pallas_call x2, Pallas kernels, cells_dft(): pl.pallas_call(partial(strike_cells_dft, sign), grid=(count,), in_specs=[...  12.4 us
    all_to_all x3, starting transfers between devices, exchange(): return lax.all_to_all(block, axis, split_axis=0, concat_axis=0)  12.1 us
    unnamed x20, local copies, waits for them, and re-layouts  8.79 us
  transfers between devices with their start and end apart: 11, of which 6 were waited for; matrix products, arithmetic and copies ran while one was open for 9% of the time, Pallas kernels for 0%

profile of v1, /device:TPU:0, one launch (start us, length us, event | category | flops | bytes accessed | tf_op | source)
XLA Modules:
  0.0 377.0 jit_solution(12437444258023069295)
XLA Ops:
  0.6 1.6 copy.130
  2.2 26.0 %all_to_all.30.x_ref = f32[8,3,32,512]{3,2,1,0:T(8,128)} all-to-all(f32[8,3,32,512]{3,2,1,0:T(8,128)S(1)} %bitcast.103), channel_id=1, replica_groups=mesh['bx'=8,'by'=4] {'bx'}, dimensions={0} | all-to-all | bytes 3145728 | tf_op jit(solution)/shard_map/all_to_all | solution.py:270
  28.3 3.9 %strike_forward.1 = f32[8,2,3,32,512]{4,3,2,1,0:T(8,128)} custom-call(f32[8,3,32,512]{3,2,1,0:T(8,128)} %all_to_all.30.x_ref), custom_call_target="tpu_custom_call" | custom-call | flops 12582912 | bytes 4718592 | tf_op jit(solution)/shard_map/strike_forward/pallas_call | solution.py:287
  32.2 3.7 all-to-all-start.1
  36.7 36.9 %all-to-all-done.1.x_ref = f32[8,2,3,32,512]{4,3,2,1,0:T(8,128)S(1)} async-done(((f32[8,2,3,32,512]{4,3,2,1,0:T(8,128)}), f32[8,2,3,32,512]{4,3,2,1,0:T(8,128)S(1)}, u32[]{:S(2)}, u32[]{:S(2)}) %all-to-all-start.1) | async-done | bytes 3145760 | tf_op jit(solution)/shard_map/all_to_all | solution.py:270
  73.6 1.7 copy-done.1
  75.3 6.3 %strike_cells.2 = f32[4,2,3,64,512]{4,3,2,1,0:T(8,128)} custom-call(f32[8,2,3,32,512]{4,3,2,1,0:T(8,128)} %copy-done.1, f32[256,2]{1,0:T(8,128)} %copy.98.tw_ref, bf16[2,2,256,256]{3,2,1,0:T(8,128)(2,1)} %constant.15.clone.table_ref), custom_call_target="tpu_custom_call" | custom-call | flops 2415919104 | bytes 6291456 | tf_op jit(solution)/shard_map/strike_cells/pallas_call | solution.py:296
  81.6 4.9 %all-to-all-start.2 = ((f32[4,2,3,64,512]{4,3,2,1,0:T(8,128)}), f32[4,2,3,64,512]{4,3,2,1,0:T(8,128)S(1)}, u32[]{:S(2)}, u32[]{:S(2)}) async-start(f32[4,2,3,64,512]{4,3,2,1,0:T(8,128)} %strike_cells.2), calls=%async_computation.2 | async-start | bytes 6291456 | tf_op jit(solution)/shard_map/all_to_all | solution.py:270
  86.5 2.8 slice_bitcast_fusion.10
  89.3 7.9 %fusion.2 = f32[2,3,4,64,512]{4,2,3,1,0:T(4,128)S(1)} fusion(f32[6,2,3,64,1,4,512]{6,5,3,2,1,4,0:T(4,128)} %bitcast.99, f32[6,2,3,64,1,4,512]{6,5,4,3,2,1,0:T(4,128)} %param.10, f32[64,4,512]{2,1,0:T(4,128)S(1)} %get-tuple-element.25, f32[64,4,512]{2,1,0:T(4,128)S(1)} %get-tuple-element.26, f32[64,4,512]{2,1,0:T(4,128)S(1)} %get-tuple-element.21, ...), kind=kLoop, calls=%fused_computation.3 | loop fusion | flops 8650752 | bytes 25165824 | tf_op jit(solution)/shard_map/transpose | solution.py:374
  97.2 2.6 copy.105
  100.8 53.5 %all-to-all-done.2.x_ref = f32[4,2,3,64,512]{4,3,2,1,0:T(8,128)S(1)} async-done(((f32[4,2,3,64,512]{4,3,2,1,0:T(8,128)}), f32[4,2,3,64,512]{4,3,2,1,0:T(8,128)S(1)}, u32[]{:S(2)}, u32[]{:S(2)}) %all-to-all-start.2) | async-done | bytes 3145760 | tf_op jit(solution)/shard_map/all_to_all | solution.py:270
  154.3 1.7 copy-done
  155.9 14.9 %dip_response.1 = f32[4,2,3,64,512]{4,3,2,1,0:T(8,128)} custom-call(f32[4,2,3,64,512]{4,3,2,1,0:T(8,128)} %copy-done, f32[2,4,512]{2,1,0:T(4,128)} %constant.14.clone.tw_ref, bf16[2,2,512,512]{3,2,1,0:T(8,128)(2,1)} %constant.16.clone.table_ref, f32[256,512]{1,0:T(8,128)} %bitcast.105, f32[2,3,256,512]{3,2,1,0:T(8,128)} %bitcast.104), custom_call_target="tpu_custom_call" | custom-call | flops 9663676416 | bytes 9961472 | tf_op jit(solution)/shard_map/dip_response/pallas_call | solution.py:312
  170.9 75.5 %all_to_all.31.x_ref = f32[4,2,3,64,512]{4,3,2,1,0:T(8,128)} all-to-all(f32[4,2,3,64,512]{4,3,2,1,0:T(8,128)} %dip_response.1), channel_id=1, replica_groups=mesh['bx'=8,'by'=4] {'by'}, dimensions={0} | all-to-all | bytes 6291456 | tf_op jit(solution)/shard_map/all_to_all | solution.py:270
  246.4 6.1 %strike_cells.3 = f32[8,2,3,32,512]{4,3,2,1,0:T(8,128)} custom-call(f32[4,2,3,64,512]{4,3,2,1,0:T(8,128)} %all_to_all.31.x_ref, f32[256,2]{1,0:T(8,128)} %copy.98.tw_ref, bf16[2,2,256,256]{3,2,1,0:T(8,128)(2,1)} %constant.15.clone.table_ref), custom_call_target="tpu_custom_call" | custom-call | flops 2415919104 | bytes 6291456 | tf_op jit(solution)/shard_map/strike_cells/pallas_call | solution.py:296
  252.5 42.8 %all_to_all.32.x_ref = f32[8,2,3,32,512]{4,3,2,1,0:T(8,128)} all-to-all(f32[8,2,3,32,512]{4,3,2,1,0:T(8,128)} %strike_cells.3), channel_id=1, replica_groups=mesh['bx'=8,'by'=4] {'bx'}, dimensions={0} | all-to-all | bytes 6291456 | tf_op jit(solution)/shard_map/all_to_all | solution.py:270
  295.2 3.9 %strike_inverse.1 = f32[8,3,32,512]{3,2,1,0:T(8,128)} custom-call(f32[8,2,3,32,512]{4,3,2,1,0:T(8,128)} %all_to_all.32.x_ref), custom_call_target="tpu_custom_call" | custom-call | flops 12582912 | bytes 4718592 | tf_op jit(solution)/shard_map/strike_inverse/pallas_call | solution.py:331
  299.1 3.6 all-to-all-start.5
  304.5 3.5 fusion.13
  309.1 1.2 copy.122
  310.4 1.2 copy.121
  311.6 1.5 collective-permute-start.3
  314.4 1.7 collective-permute-start.1
  316.1 3.2 collective-permute-done.2
  320.1 3.8 %all-to-all-done.5 = f32[8,3,32,512]{3,2,1,0:T(8,128)S(1)} async-done(((f32[8,3,32,512]{3,2,1,0:T(8,128)}), f32[8,3,32,512]{3,2,1,0:T(8,128)S(1)}, u32[]{:S(2)}, u32[]{:S(2)}) %all-to-all-start.5) | async-done | bytes 1572896 | tf_op jit(solution)/shard_map/all_to_all | solution.py:270
  323.9 1.3 copy.107
  325.8 17.0 %velocity_step.1 = (f32[3,4,256,512]{3,2,1,0:T(8,128)}, f32[256,24]{1,0:T(8,128)}) custom-call(f32[6,4,256,512]{3,2,1,0:T(8,128)} %s_ref.3, f32[6,4,256,512]{3,2,1,0:T(8,128)} %s_ref.3, f32[6,4,256,512]{3,2,1,0:T(8,128)} %s_ref.3, f32[3,4,512]{2,1,0:T(4,128)} %copy-done.2, f32[3,4,512]{2,1,0:T(4,128)} %copy-done.3, f32[256,24]{1,0:T(8,128)} %copy.108.col_ref, ...), custom_call_target="tpu_custom_call" | custom-call | flops 10000000 | bytes 25165824 | tf_op jit(solution)/shard_map/velocity_step/pallas_call | solution.py:406
  344.2 3.6 collective-permute-start.7
  347.8 6.8 %copy.109 = f32[3,4,256,512]{3,1,0,2:T(4,128)S(1)} copy(f32[3,4,256,512]{3,2,1,0:T(8,128)} %get-tuple-element.2.v_ref.prev_ref.next_ref) | data formatting | bytes 12582912 | tf_op jit(solution)/shard_map/velocity_step/pallas_call | solution.py:406
  356.2 2.7 collective-permute-done.4.low_ref
  359.5 17.4 %stress_step.1 = f32[6,4,256,512]{3,2,1,0:T(8,128)} custom-call(f32[3,4,256,512]{3,2,1,0:T(8,128)} %get-tuple-element.2.v_ref.prev_ref.next_ref, f32[3,4,256,512]{3,2,1,0:T(8,128)} %get-tuple-element.2.v_ref.prev_ref.next_ref, f32[3,4,256,512]{3,2,1,0:T(8,128)} %get-tuple-element.2.v_ref.prev_ref.next_ref, f32[3,4,512]{2,1,0:T(4,128)} %copy-done.5, ...), custom_call_target="tpu_custom_call" | custom-call | flops 20000000 | bytes 31457280 | tf_op jit(solution)/shard_map/stress_step/pallas_call | solution.py:426
  (43 shorter events, 10.9 us)
Async XLA Ops:
  32.2 41.4 %all-to-all-start.1 = ((f32[8,2,3,32,512]{4,3,2,1,0:T(8,128)}), f32[8,2,3,32,512]{4,3,2,1,0:T(8,128)S(1)}, u32[]{:S(2)}, u32[]{:S(2)}) async-start(f32[8,2,3,32,512]{4,3,2,1,0:T(8,128)} %strike_forward.1), calls=%async_computation.1 | async-start | bytes 6291456 | tf_op jit(solution)/shard_map/all_to_all | solution.py:270
  73.6 1.7 copy-start.1
  81.6 72.7 %all-to-all-start.2 = ((f32[4,2,3,64,512]{4,3,2,1,0:T(8,128)}), f32[4,2,3,64,512]{4,3,2,1,0:T(8,128)S(1)}, u32[]{:S(2)}, u32[]{:S(2)}) async-start(f32[4,2,3,64,512]{4,3,2,1,0:T(8,128)} %strike_cells.2), calls=%async_computation.2 | async-start | bytes 6291456 | tf_op jit(solution)/shard_map/all_to_all | solution.py:270
  154.3 1.7 copy-start
  299.1 24.8 %all-to-all-start.5 = ((f32[8,3,32,512]{3,2,1,0:T(8,128)}), f32[8,3,32,512]{3,2,1,0:T(8,128)S(1)}, u32[]{:S(2)}, u32[]{:S(2)}) async-start(f32[8,3,32,512]{3,2,1,0:T(8,128)} %strike_inverse.1), calls=%async_computation.5 | async-start | bytes 3145728 | tf_op jit(solution)/shard_map/all_to_all | solution.py:270
  303.8 21.4 %collective-permute-start = (f32[3,4,512]{2,1,0:T(4,128)S(1)}, f32[3,4,512]{2,1,0:T(4,128)S(1)}, u32[]{:S(2)}, u32[]{:S(2)}) collective-permute-start(f32[3,4,512]{2,1,0:T(4,128)S(1)} %pad_maximum_fusion.1), channel_id=1, source_target_pairs={{0,4},{4,8},{8,12},{12,16},{16,20},{20,24},{24,28},{28,0},{1,5},{5... | collective-permute-start | bytes 73736 | tf_op jit(solution)/shard_map/ppermute | solution.py:275
  311.6 4.5 %collective-permute-start.3 = (f32[256,12]{0,1:T(8,128)S(1)}, f32[256,12]{0,1:T(8,128)S(1)}, u32[]{:S(2)}, u32[]{:S(2)}) collective-permute-start(f32[256,12]{0,1:T(8,128)S(1)} %maximum_bitcast_fusion.1), channel_id=1, source_target_pairs={{1,0},{2,1},{3,2},{0,3},{5,4},{6,5},{7,6},{4,7},{9,8},{10,9},{11,1... | collective-permute-start | bytes 36872 | tf_op jit(solution)/shard_map/ppermute | solution.py:275
  313.7 5.6 %collective-permute-start.2 = (f32[256,12]{0,1:T(8,128)S(1)}, f32[256,12]{0,1:T(8,128)S(1)}, u32[]{:S(2)}, u32[]{:S(2)}) collective-permute-start(f32[256,12]{0,1:T(8,128)S(1)} %maximum_bitcast_fusion), channel_id=1, source_target_pairs={{0,1},{1,2},{2,3},{3,0},{4,5},{5,6},{6,7},{7,4},{8,9},{9,10},{10,1... | collective-permute-start | bytes 36872 | tf_op jit(solution)/shard_map/ppermute | solution.py:275
  314.4 10.9 %collective-permute-start.1 = (f32[3,4,512]{2,1,0:T(4,128)S(1)}, f32[3,4,512]{2,1,0:T(4,128)S(1)}, u32[]{:S(2)}, u32[]{:S(2)}) collective-permute-start(f32[3,4,512]{2,1,0:T(4,128)S(1)} %pad_maximum_fusion.2), channel_id=1, source_target_pairs={{4,0},{8,4},{12,8},{16,12},{20,16},{24,20},{28,24},{0,28},{5,1},{9... | collective-permute-start | bytes 73736 | tf_op jit(solution)/shard_map/ppermute | solution.py:275
  325.2 0.6 copy-start.2
  325.2 0.6 copy-start.3
  343.9 11.3 %collective-permute-start.6 = (f32[256,12]{1,0:T(8,128)S(1)}, f32[256,12]{1,0:T(8,128)S(1)}, u32[]{:S(2)}, u32[]{:S(2)}) collective-permute-start(f32[256,12]{1,0:T(8,128)S(1)} %get-tuple-element.27), channel_id=1, source_target_pairs={{0,1},{1,2},{2,3},{3,0},{4,5},{5,6},{6,7},{7,4},{8,9},{9,10},{10,1... | collective-permute-start | bytes 36872 | tf_op jit(solution)/shard_map/ppermute | solution.py:275
  344.2 11.0 %collective-permute-start.7 = (f32[256,12]{1,0:T(8,128)S(1)}, f32[256,12]{1,0:T(8,128)S(1)}, u32[]{:S(2)}, u32[]{:S(2)}) collective-permute-start(f32[256,12]{1,0:T(8,128)S(1)} %get-tuple-element.28), channel_id=1, source_target_pairs={{1,0},{2,1},{3,2},{0,3},{5,4},{6,5},{7,6},{4,7},{9,8},{10,9},{11,1... | collective-permute-start | bytes 36872 | tf_op jit(solution)/shard_map/ppermute | solution.py:275
  354.6 1.6 collective-permute-start.5
  354.7 4.2 %collective-permute-start.4 = (f32[3,4,512]{2,1,0:T(4,128)S(1)}, f32[3,4,512]{2,1,0:T(4,128)S(1)}, u32[]{:S(2)}, u32[]{:S(2)}) collective-permute-start(f32[3,4,512]{2,1,0:T(4,128)S(1)} %get-tuple-element.19), channel_id=1, source_target_pairs={{0,4},{4,8},{8,12},{12,16},{16,20},{20,24},{24,28},{28,0},{1,5},{5... | collective-permute-start | bytes 73736 | tf_op jit(solution)/shard_map/ppermute | solution.py:275
  356.2 2.7 copy-start.4
  358.9 0.6 copy-start.5

commit v2 on v1

--- a/solution.py
+++ b/solution.py
@@ -11,7 +11,6 @@
 
 COURANT = 0.3
 FRICTION = 0.6
-CHUNKS = 1
 F32 = jnp.float32
 BF16 = jnp.bfloat16
 
@@ -66,33 +65,31 @@
 
 
 def strike_forward(count, x_ref, o_ref):
-    for c in range(x_ref.shape[1]):
+    for r in range(count):
+        real_part = imag_part = None
+        for b in range(count):
+            cos, sin = root(r * b, count)
+            real_part = add_term(real_part, cos, x_ref[b])
+            imag_part = add_term(imag_part, -sin, x_ref[b])
+        o_ref[r, 0] = real_part
+        o_ref[r, 1] = jnp.zeros_like(real_part) if imag_part is None else imag_part
+
+
+def strike_inverse(count, scale, x_ref, o_ref):
+    for b in range(count):
+        total = None
         for r in range(count):
-            real_part = imag_part = None
-            for b in range(count):
-                cos, sin = root(r * b, count)
-                real_part = add_term(real_part, cos, x_ref[b, c])
-                imag_part = add_term(imag_part, -sin, x_ref[b, c])
-            o_ref[r, 0, c] = real_part
-            o_ref[r, 1, c] = jnp.zeros_like(real_part) if imag_part is None else imag_part
-
-
-def strike_inverse(count, scale, x_ref, o_ref):
-    for c in range(x_ref.shape[2]):
-        for b in range(count):
-            total = None
-            for r in range(count):
-                cos, sin = root(r * b, count)
-                total = add_term(total, cos, x_ref[r, 0, c])
-                total = add_term(total, -sin, x_ref[r, 1, c])
-            o_ref[b, c] = scale * total
+            cos, sin = root(r * b, count)
+            total = add_term(total, cos, x_ref[r, 0])
+            total = add_term(total, -sin, x_ref[r, 1])
+        o_ref[b] = scale * total
 
 
 def strike_cells_dft(sign, x_ref, tw_ref, table_ref, o_ref, held):
-    blocks, _, _, rows, _ = x_ref.shape
+    blocks, _, rows, _ = x_ref.shape
     for s in range(blocks):
         for z in range(2):
-            held[z, pl.ds(s * rows, rows), :] = x_ref[s, z, 0]
+            held[z, pl.ds(s * rows, rows), :] = x_ref[s, z]
     cos, sin = tw_ref[:, 0:1], sign * tw_ref[:, 1:2]
     real_part, imag_part = held[0], held[1]
     if sign < 0:
@@ -108,29 +105,29 @@
         )
     held[0] = real_part
     held[1] = imag_part
-    blocks, _, _, rows, _ = o_ref.shape
+    blocks, _, rows, _ = o_ref.shape
     for s in range(blocks):
         for z in range(2):
-            o_ref[s, z, 0] = held[z, pl.ds(s * rows, rows), :]
+            o_ref[s, z] = held[z, pl.ds(s * rows, rows), :]
 
 
 def dip_response(scale, x_ref, tw_ref, table_ref, now_ref, past_ref, o_ref, held):
-    count, _, _, rows, _ = x_ref.shape
+    count, _, rows, _ = x_ref.shape
     for l in range(count):
         real_part = imag_part = None
         for j in range(count):
             cos, sin = root(l * j, count)
-            real_part = add_term(real_part, cos, x_ref[j, 0, 0])
-            real_part = add_term(real_part, sin, x_ref[j, 1, 0])
-            imag_part = add_term(imag_part, cos, x_ref[j, 1, 0])
-            imag_part = add_term(imag_part, -sin, x_ref[j, 0, 0])
+            real_part = add_term(real_part, cos, x_ref[j, 0])
+            real_part = add_term(real_part, sin, x_ref[j, 1])
+            imag_part = add_term(imag_part, cos, x_ref[j, 1])
+            imag_part = add_term(imag_part, -sin, x_ref[j, 0])
         cos, sin = tw_ref[0, l : l + 1, :], tw_ref[1, l : l + 1, :]
         held[0, pl.ds(l * rows, rows), :] = real_part * cos + imag_part * sin
         held[1, pl.ds(l * rows, rows), :] = imag_part * cos - real_part * sin
     real_part, imag_part = complex_product(held[0], held[1], table_ref, -1.0, False)
     weight = scale * now_ref[...]
-    real_part = weight * real_part + past_ref[0, 0]
-    imag_part = weight * imag_part + past_ref[1, 0]
+    real_part = weight * real_part + past_ref[0]
+    imag_part = weight * imag_part + past_ref[1]
     real_part, imag_part = complex_product(real_part, imag_part, table_ref, 1.0, False)
     held[0] = real_part
     held[1] = imag_part
@@ -150,8 +147,8 @@
             real_part = add_term(real_part, -sin, li)
             imag_part = add_term(imag_part, cos, li)
             imag_part = add_term(imag_part, sin, lr)
-        o_ref[j, 0, 0] = real_part
-        o_ref[j, 1, 0] = imag_part
+        o_ref[j, 0] = real_part
+        o_ref[j, 1] = imag_part
 
 
 def rows_diff(value, before, after):
@@ -170,11 +167,6 @@
     return 0.5 * (high - low)
 
 
-def layer_diff(layers, ghost, z):
-    low = ghost if z == 0 else layers(z - 1)
-    return 0.5 * (layers(z + 1) - low)
-
-
 def strike_edges(low_ref, prev_ref, high_ref, next_ref, slot, component, z):
     i, last = pl.program_id(0), pl.num_programs(0) - 1
     before = jnp.where(i == 0, low_ref[slot, z : z + 1, :], prev_ref[component, z, 7:8, :])
@@ -182,7 +174,7 @@
     return before, after
 
 
-def velocity_step(s_ref, prev_ref, next_ref, low_ref, high_ref, col_ref, v_ref, t_ref, o_ref, c_ref):
+def velocity_step(s_ref, prev_ref, next_ref, low_ref, high_ref, col_ref, v_ref, t_ref, o_ref, c_ref, l_ref, h_ref):
     layers = v_ref.shape[1]
     width = v_ref.shape[3]
     half = 3 * layers
@@ -203,6 +195,14 @@
             o_ref[component, z] = value
             c_ref[:, k : k + 1] = value[:, 0:1]
             c_ref[:, half + k : half + k + 1] = value[:, width - 1 : width]
+
+            @pl.when(pl.program_id(0) == 0)
+            def _():
+                l_ref[component, z : z + 1, :] = value[0:1, :]
+
+            @pl.when(pl.program_id(0) == pl.num_programs(0) - 1)
+            def _():
+                h_ref[component, z : z + 1, :] = value[-1:, :]
 
 
 def stress_step(v_ref, prev_ref, next_ref, low_ref, high_ref, col_ref, w_ref, s_ref, y_ref, o_ref):
@@ -246,11 +246,6 @@
     return pl.BlockSpec(shape, lambda *_: (0,) * len(shape))
 
 
-def component_block(shape, dim):
-    block = tuple(1 if d == dim else n for d, n in enumerate(shape))
-    return pl.BlockSpec(block, lambda c: tuple(c if d == dim else 0 for d in range(len(shape))))
-
-
 def struct(shape):
     return jax.ShapeDtypeStruct(shape, F32)
 
@@ -266,76 +261,155 @@
     return forward, [(b, a) for a, b in forward]
 
 
-def exchange(block, axis):
-    return lax.all_to_all(block, axis, split_axis=0, concat_axis=0)
-
-
 def edges(first, last, axis):
     forward, backward = ring(axis)
     return lax.ppermute(last, axis, forward), lax.ppermute(first, axis, backward)
+
+
+def fault_kernel(
+    scale,
+    face_ref,
+    strike_tw_ref,
+    strike_table_ref,
+    dip_tw_ref,
+    dip_table_ref,
+    now_ref,
+    past_ref,
+    o_ref,
+    x1,
+    b1,
+    b2,
+    t1,
+    t2,
+    u1,
+    u2,
+    w1,
+    w2,
+    y1,
+    held,
+    send_sem,
+    recv_sem,
+):
+    count = face_ref.shape[0]
+    sizes = {"bx": lax.axis_size("bx"), "by": lax.axis_size("by")}
+    place = {"bx": lax.axis_index("bx"), "by": lax.axis_index("by")}
+
+    def device(axis, target):
+        if axis == "bx":
+            return (target, place["by"])
+        return (place["bx"], target)
+
+    barrier = pltpu.get_barrier_semaphore()
+    for axis in ("bx", "by"):
+
+        @pl.loop(1, sizes[axis])
+        def _(k):
+            target = lax.rem(place[axis] + k, sizes[axis])
+            pl.semaphore_signal(
+                barrier, 1, device_id=device(axis, target), device_id_type=pl.DeviceIdType.MESH
+            )
+
+    pl.semaphore_wait(barrier, sizes["bx"] + sizes["by"] - 2)
+
+    def copy(stage, axis, c, k, source, landing):
+        me = place[axis]
+        target = lax.rem(me + k, sizes[axis])
+        return pltpu.make_async_remote_copy(
+            src_ref=source.at[c, target],
+            dst_ref=landing.at[c, me],
+            send_sem=send_sem.at[stage, c, k],
+            recv_sem=recv_sem.at[stage, c, k],
+            device_id=device(axis, target),
+            device_id_type=pl.DeviceIdType.MESH,
+        )
+
+    def own(stage, axis, c, source, landing):
+        me = place[axis]
+        return pltpu.make_async_copy(
+            source.at[c, me], landing.at[c, me], recv_sem.at[stage, c, 0]
+        )
+
+    def send(stage, axis, c, source, landing):
+        @pl.loop(1, sizes[axis])
+        def _(k):
+            copy(stage, axis, c, k, source, landing).start()
+
+        own(stage, axis, c, source, landing).start()
+
+    def receive(stage, axis, c, source, landing):
+        own(stage, axis, c, source, landing).wait()
+
+        @pl.loop(1, sizes[axis])
+        def _(k):
+            copy(stage, axis, c, k, source, landing).wait()
+
+    stages = (
+        ("bx", face_ref, x1),
+        ("bx", b1, b2),
+        ("by", t1, t2),
+        ("by", u1, u2),
+        ("bx", w1, w2),
+        ("bx", y1, o_ref),
+    )
+
+    @pl.loop(0, count)
+    def _(c):
+        send(0, stages[0][0], c, *stages[0][1:])
+
+    def work(stage, c):
+        if stage == 0:
+            strike_forward(sizes["bx"], x1.at[c], b1.at[c])
+        elif stage == 1:
+            strike_cells_dft(-1.0, b2.at[c], strike_tw_ref, strike_table_ref, t1.at[c], held)
+        elif stage == 2:
+            dip_response(
+                scale, t2.at[c], dip_tw_ref, dip_table_ref, now_ref, past_ref.at[c], u1.at[c], held
+            )
+        elif stage == 3:
+            strike_cells_dft(1.0, u2.at[c], strike_tw_ref, strike_table_ref, w1.at[c], held)
+        else:
+            strike_inverse(sizes["bx"], scale, w2.at[c], y1.at[c])
+
+    for stage in range(5):
+
+        @pl.loop(0, count)
+        def _(c):
+            receive(stage, stages[stage][0], c, *stages[stage][1:])
+            work(stage, c)
+            send(stage + 1, stages[stage + 1][0], c, *stages[stage + 1][1:])
+
+    @pl.loop(0, count)
+    def _(c):
+        receive(5, stages[5][0], c, *stages[5][1:])
 
 
 def fault_traction(interface, now, past, tables, scale):
     strike_count, dip_count = lax.axis_size("bx"), lax.axis_size("by")
     count, cells, width = interface.shape
     rows, modes = cells // strike_count, cells // dip_count
-    strike_tw, strike_table, dip_tw, dip_table = tables
-    block = interface.reshape(count, strike_count, rows, width).transpose(1, 0, 2, 3)
-    block = exchange(block, "bx")
-    wide = struct((strike_count, 2, count, rows, width))
-    tall = struct((dip_count, 2, count, modes, width))
-    block = pl.pallas_call(
-        partial(strike_forward, strike_count),
-        out_shape=wide,
-        cost_estimate=cost(wide.size * 2 * strike_count, block, wide),
-        name="strike_forward",
-    )(block)
-    block = exchange(block, "bx")
-
-    def cells_dft(block, sign, out):
-        return pl.pallas_call(
-            partial(strike_cells_dft, sign),
-            grid=(count,),
-            in_specs=[
-                component_block(block.shape, 2),
-                whole_block(strike_tw.shape),
-                whole_block(strike_table.shape),
-            ],
-            out_specs=component_block(out.shape, 2),
-            out_shape=out,
-            scratch_shapes=[pltpu.VMEM((2, cells, width), F32)],
-            cost_estimate=cost(24 * count * cells * cells * width, block, out),
-            name="strike_cells",
-        )(block, strike_tw, strike_table)
-
-    block = exchange(cells_dft(block, -1.0, tall), "by")
-    block = pl.pallas_call(
-        partial(dip_response, scale),
-        grid=(count,),
-        in_specs=[
-            component_block(block.shape, 2),
-            whole_block(dip_tw.shape),
-            whole_block(dip_table.shape),
-            whole_block(now.shape),
-            component_block(past.shape, 1),
+    flat = (count, strike_count, rows, width)
+    wide = (count, strike_count, 2, rows, width)
+    tall = (count, dip_count, 2, modes, width)
+    peers = max(strike_count, dip_count)
+    operands = (interface.reshape(flat), *tables, now, past)
+    out = pl.pallas_call(
+        partial(fault_kernel, scale),
+        out_shape=struct(flat),
+        in_specs=[pl.BlockSpec(memory_space=pltpu.VMEM)] * len(operands),
+        out_specs=pl.BlockSpec(memory_space=pltpu.VMEM),
+        scratch_shapes=[
+            *[pltpu.VMEM(s, F32) for s in (flat, wide, wide, tall, tall, tall, tall, wide, wide)],
+            pltpu.VMEM(flat, F32),
+            pltpu.VMEM((2, cells, width), F32),
+            pltpu.SemaphoreType.DMA((6, count, peers)),
+            pltpu.SemaphoreType.DMA((6, count, peers)),
         ],
-        out_specs=component_block(tall.shape, 2),
-        out_shape=tall,
-        scratch_shapes=[pltpu.VMEM((2, cells, width), F32)],
-        cost_estimate=cost(48 * count * cells * width * width, block, tall, past, now),
-        name="dip_response",
-    )(block, dip_tw, dip_table, now, past)
-    block = exchange(block, "by")
-    block = exchange(cells_dft(block, 1.0, wide), "bx")
-    flat = struct((strike_count, count, rows, width))
-    block = pl.pallas_call(
-        partial(strike_inverse, strike_count, scale),
-        out_shape=flat,
-        cost_estimate=cost(wide.size * 2 * strike_count, block, flat),
-        name="strike_inverse",
-    )(block)
-    block = exchange(block, "bx")
-    return block.transpose(1, 0, 2, 3).reshape(count, cells, width)
+        compiler_params=pltpu.CompilerParams(
+            collective_id=0, has_side_effects=True, vmem_limit_bytes=60 * 1024 * 1024
+        ),
+        name="fault_traction",
+    )(*operands)
+    return out.reshape(count, cells, width)
 
 
 def tile_spec(shape, tile):
@@ -371,20 +445,11 @@
     for h in range(1, history.shape[0]):
         past = past + kernel[h + 1] * history[h]
     modes = history.shape[3]
-    past = past.reshape(2, 3, modes, dip_count, width).transpose(0, 1, 3, 2, 4)
-    past = past.reshape(2, 3, cells, width)
+    past = past.reshape(2, 3, modes, dip_count, width).transpose(1, 0, 3, 2, 4)
+    past = past.reshape(3, 2, cells, width)
     now = kernel[0].reshape(modes, dip_count, width).transpose(1, 0, 2).reshape(cells, width)
 
-    step = 3 // CHUNKS
-    traction = jnp.concatenate(
-        [
-            fault_traction(
-                interface_velocity[c : c + step], now, past[:, c : c + step], tables, scale
-            )
-            for c in range(0, 3, step)
-        ],
-        axis=0,
-    )
+    traction = fault_traction(interface_velocity, now, past, tables, scale)
 
     tile = min(32, cells)
     grid = (cells // tile,)
@@ -403,7 +468,7 @@
 
     cols = columns(side(0), side(width - 1))
     low, high = edges(line(0), line(cells - 1), "bx")
-    velocity_new, new_cols = pl.pallas_call(
+    velocity_new, new_cols, first, last = pl.pallas_call(
         velocity_step,
         grid=grid,
         in_specs=[
@@ -415,14 +480,19 @@
             tile_spec(velocity.shape, tile),
             tile_spec(traction.shape, tile),
         ],
-        out_specs=[tile_spec(velocity.shape, tile), tile_spec(col_shape, tile)],
-        out_shape=[struct(velocity.shape), struct(col_shape)],
+        out_specs=[
+            tile_spec(velocity.shape, tile),
+            tile_spec(col_shape, tile),
+            whole_block(low.shape),
+            whole_block(low.shape),
+        ],
+        out_shape=[struct(velocity.shape), struct(col_shape), struct(low.shape), struct(low.shape)],
         cost_estimate=cost(1e7, stress, velocity, velocity),
         name="velocity_step",
     )(stress, stress, stress, low, high, cols, velocity, traction)
     half = 3 * layers
     cols = columns(new_cols[:, :half], new_cols[:, half:])
-    low, high = edges(velocity_new[:, :, 0], velocity_new[:, :, cells - 1], "bx")
+    low, high = edges(first, last, "bx")
     stress_new = pl.pallas_call(
         stress_step,
         grid=grid,

time: 378 us -> 290 us (0.77)
  Pallas kernels: 69.6 us -> 241 us
  blocking collectives: 144 us -> 0 us
  waiting for transfers between devices: 100 us -> 4.46 us
  local copies, waits for them, and re-layouts: 32 us -> 15.7 us
    pallas_call x5 -> x1, Pallas kernels: 35.1 us -> 203 us  [fault_traction(): pl.pallas_call(partial(fault_kernel, scale), out_shape=struct(flat), in_s...]
    all_to_all x3 -> x0, blocking collectives: 144 us -> none  [exchange(): return lax.all_to_all(block, axis, split_axis=0, concat_axis=0)]
    all_to_all x3 -> x0, waiting for transfers between devices: 94.2 us -> none  [exchange(): return lax.all_to_all(block, axis, split_axis=0, concat_axis=0)]
    all_to_all x3 -> x0, starting transfers between devices: 12.1 us -> none  [exchange(): return lax.all_to_all(block, axis, split_axis=0, concat_axis=0)]
    pallas_call x1 -> x0, local copies, waits for them, and re-layouts: 6.83 us -> none  [local(): pl.pallas_call(velocity_step, grid=grid, in_specs=[tile_spec(stress.shape...]
    unnamed x20 -> x18, local copies, waits for them, and re-layouts: 8.79 us -> 2.36 us
    ppermute x4, starting transfers between devices: 2.01 us -> 7.73 us  [edges(): lax.ppermute(last, axis, forward)]
    ppermute x4, waiting for transfers between devices: 5.89 us -> 1.24 us  [edges(): lax.ppermute(last, axis, forward)]
  transfers between devices with their start and end apart: 11 -> 8, of which waited for: 6 -> 2; matrix products, arithmetic and copies ran while one was open for 9% -> 7% of each run, Pallas kernels for 0% -> 70%
where the time goes in v2:
time: 290 us
  Pallas kernels  241 us (83%)
  starting transfers between devices  18.6 us (6%)
  local copies, waits for them, and re-layouts  15.7 us (5%)
  other arithmetic  8.78 us (3%)
  waiting for transfers between devices  4.46 us (2%)
    pallas_call x1, Pallas kernels, fault_traction(): pl.pallas_call(partial(fault_kernel, scale), out_shape=struct(flat), in_s...  203 us
    pallas_call x1, Pallas kernels, local(): pl.pallas_call(velocity_step, grid=grid, in_specs=[tile_spec(stress.shape...  20.8 us
    pallas_call x1, Pallas kernels, local(): pl.pallas_call(stress_step, grid=grid, in_specs=[tile_spec(velocity.shape...  17.5 us
    ppermute x4, starting transfers between devices, edges(): lax.ppermute(first, axis, backward)  10.9 us
    transpose x1, other arithmetic, local(): past = past.reshape(2, 3, modes, dip_count, width).transpose(1, 0, 3, 2, 4)  7.91 us
    ppermute x4, starting transfers between devices, edges(): lax.ppermute(last, axis, forward)  7.73 us
  transfers between devices with their start and end apart: 8, of which 2 were waited for; matrix products, arithmetic and copies ran while one was open for 7% of the time, Pallas kernels for 70%

profile of v2, /device:TPU:0, one launch (start us, length us, event | category | flops | bytes accessed | tf_op | source)
XLA Modules:
  0.0 289.5 jit_solution(13030725178932585125)
XLA Ops:
  0.6 1.0 fusion.14
  1.7 0.5 collective-permute-start
  2.3 2.9 %collective-permute-start.1 = (f32[3,4,512]{2,1,0:T(4,128)S(1)}, f32[3,4,512]{2,1,0:T(4,128)S(1)}, u32[]{:S(2)}, u32[]{:S(2)}) collective-permute-start(f32[3,4,512]{2,1,0:T(4,128)S(1)} %pad_maximum_fusion.2), channel_id=1, source_target_pairs={{4,0},{8,4},{12,8},{16,12},{20,16},{24,20},{28,24},{0,28},{5,1},{9... | collective-permute-start | bytes 73736 | tf_op jit(solution)/shard_map/ppermute | solution.py:266
  5.2 2.4 fusion.13
  7.7 0.2 copy.84
  7.8 0.2 copy.86
  8.0 0.2 copy.85
  8.3 4.4 %collective-permute-start.3 = (f32[256,12]{0,1:T(8,128)S(1)}, f32[256,12]{0,1:T(8,128)S(1)}, u32[]{:S(2)}, u32[]{:S(2)}) collective-permute-start(f32[256,12]{0,1:T(8,128)S(1)} %maximum_bitcast_fusion.1), channel_id=1, source_target_pairs={{1,0},{2,1},{3,2},{0,3},{5,4},{6,5},{7,6},{4,7},{9,8},{10,9},{11,1... | collective-permute-start | bytes 36872 | tf_op jit(solution)/shard_map/ppermute | solution.py:266
  12.6 0.2 copy.81
  12.8 0.2 copy.83
  13.0 0.2 copy.82
  13.2 0.1 collective-permute-start.2
  13.3 0.1 fusion.11
  13.4 3.6 %slice_bitcast_fusion.10 = (f32[64,4,512]{2,1,0:T(4,128)S(1)}, f32[64,4,512]{2,1,0:T(4,128)S(1)}, f32[64,4,512]{2,1,0:T(4,128)S(1)}, f32[64,4,512]{2,1,0:T(4,128...) fusion(f32[7,64,1,4,512]{4,3,2,1,0:T(4,128)} %param.11), kind=kLoop, calls=%fused_computation.22 | loop fusion | bytes 7340032 | tf_op jit(solution)/shard_map/mul | solution.py:444
  17.0 7.9 %fusion.2 = f32[3,2,4,64,512]{4,2,3,0,1:T(4,128)S(1)} fusion(f32[6,2,3,64,1,4,512]{6,5,3,2,1,4,0:T(4,128)} %bitcast.91, f32[6,2,3,64,1,4,512]{6,5,4,3,2,1,0:T(4,128)} %param.10, f32[64,4,512]{2,1,0:T(4,128)S(1)} %get-tuple-element.27, f32[64,4,512]{2,1,0:T(4,128)S(1)} %get-tuple-element.28, f32[64,4,512]{2,1,0:T(4,128)S(1)} %get-tuple-element.23, ...), kind=kLoop, calls=%fused_computation.3 | loop fusion | flops 8650752 | bytes 25165824 | tf_op jit(solution)/shard_map/transpose | solution.py:448
  24.9 0.8 copy.73.strike_tw_ref
  25.8 2.6 copy.72
  28.4 1.0 copy.66
  29.4 202.9 %fault_traction.1 = f32[3,8,32,512]{3,2,1,0:T(8,128)} custom-call(f32[3,8,32,512]{3,2,1,0:T(8,128)} %bitcast.93, f32[256,2]{1,0:T(8,128)} %copy.73.strike_tw_ref, bf16[2,2,256,256]{3,2,1,0:T(8,128)(2,1)} %constant.15.clone.strike_table_ref, f32[2,4,512]{2,1,0:T(4,128)} %constant.14.clone.dip_tw_ref, bf16[2,2,512,512]{3,2,1,0:T(8,128)(2,1)} %constant.16.clone.dip_table_ref, ...), custom_call_target="tpu_custom_call" | custom-call | tf_op jit(solution)/shard_map/fault_traction/pallas_call | solution.py:395
  232.3 0.8 copy.74.col_ref
  233.1 0.6 copy-done.1
  233.7 20.8 %velocity_step.1 = (f32[3,4,256,512]{3,2,1,0:T(8,128)}, f32[256,24]{1,0:T(8,128)}, f32[3,4,512]{2,1,0:T(4,128)}, f32[3,4,512]{2,1,0:T(4,128)}) custom-call(f32[6,4,256,512]{3,2,1,0:T(8,128)} %s_ref.3, f32[6,4,256,512]{3,2,1,0:T(8,128)} %s_ref.3, f32[6,4,256,512]{3,2,1,0:T(8,128)} %s_ref.3, f32[3,4,512]{2,1,0:T(4,128)} %copy-done.1, f32[3,4,512]{2,1,0:T(4,128)} %copy-done.2, ...), custom_call_target="tpu_custom_call" | custom-call | flops 10000000 | bytes 25165824 | tf_op jit(solution)/shard_map/velocity_step/pallas_call | solution.py:471
  254.5 1.1 fusion.15
  255.5 6.2 %collective-permute-start.6 = (f32[256,12]{1,0:T(8,128)S(1)}, f32[256,12]{1,0:T(8,128)S(1)}, u32[]{:S(2)}, u32[]{:S(2)}) collective-permute-start(f32[256,12]{1,0:T(8,128)S(1)} %get-tuple-element.29), channel_id=1, source_target_pairs={{0,1},{1,2},{2,3},{3,0},{4,5},{5,6},{6,7},{7,4},{8,9},{9,10},{10,1... | collective-permute-start | bytes 36872 | tf_op jit(solution)/shard_map/ppermute | solution.py:266
  261.8 1.8 collective-permute-start.7
  263.6 0.9 collective-permute-start.4
  264.5 1.7 collective-permute-start.5
  266.2 1.2 collective-permute-done.6
  267.5 3.2 %collective-permute-done.7 = f32[256,12]{1,0:T(8,128)S(1)} collective-permute-done((f32[256,12]{1,0:T(8,128)S(1)}, f32[256,12]{1,0:T(8,128)S(1)}, u32[]{:S(2)}, u32[]{:S(2)}) %collective-permute-start.7) | collective-permute-done | bytes 12320 | tf_op jit(solution)/shard_map/ppermute | solution.py:266
  270.7 0.8 pad_maximum_fusion.col_ref
  271.5 0.6 copy-done.3
  272.1 17.5 %stress_step.1 = f32[6,4,256,512]{3,2,1,0:T(8,128)} custom-call(f32[3,4,256,512]{3,2,1,0:T(8,128)} %get-tuple-element.4.v_ref.prev_ref.next_ref, f32[3,4,256,512]{3,2,1,0:T(8,128)} %get-tuple-element.4.v_ref.prev_ref.next_ref, f32[3,4,256,512]{3,2,1,0:T(8,128)} %get-tuple-element.4.v_ref.prev_ref.next_ref, f32[3,4,512]{2,1,0:T(4,128)} %copy-done.3, ...), custom_call_target="tpu_custom_call" | custom-call | flops 20000000 | bytes 31457280 | tf_op jit(solution)/shard_map/stress_step/pallas_call | solution.py:496
  (24 shorter events, 0.1 us)
Async XLA Ops:
  1.7 231.3 %collective-permute-start = (f32[3,4,512]{2,1,0:T(4,128)S(1)}, f32[3,4,512]{2,1,0:T(4,128)S(1)}, u32[]{:S(2)}, u32[]{:S(2)}) collective-permute-start(f32[3,4,512]{2,1,0:T(4,128)S(1)} %pad_maximum_fusion.1), channel_id=1, source_target_pairs={{0,4},{4,8},{8,12},{12,16},{16,20},{20,24},{24,28},{28,0},{1,5},{5... | collective-permute-start | bytes 73736 | tf_op jit(solution)/shard_map/ppermute | solution.py:266
  2.3 230.8 %collective-permute-start.1 = (f32[3,4,512]{2,1,0:T(4,128)S(1)}, f32[3,4,512]{2,1,0:T(4,128)S(1)}, u32[]{:S(2)}, u32[]{:S(2)}) collective-permute-start(f32[3,4,512]{2,1,0:T(4,128)S(1)} %pad_maximum_fusion.2), channel_id=1, source_target_pairs={{4,0},{8,4},{12,8},{16,12},{20,16},{24,20},{28,24},{0,28},{5,1},{9... | collective-permute-start | bytes 73736 | tf_op jit(solution)/shard_map/ppermute | solution.py:266
  8.3 224.0 %collective-permute-start.3 = (f32[256,12]{0,1:T(8,128)S(1)}, f32[256,12]{0,1:T(8,128)S(1)}, u32[]{:S(2)}, u32[]{:S(2)}) collective-permute-start(f32[256,12]{0,1:T(8,128)S(1)} %maximum_bitcast_fusion.1), channel_id=1, source_target_pairs={{1,0},{2,1},{3,2},{0,3},{5,4},{6,5},{7,6},{4,7},{9,8},{10,9},{11,1... | collective-permute-start | bytes 36872 | tf_op jit(solution)/shard_map/ppermute | solution.py:266
  13.2 219.0 %collective-permute-start.2 = (f32[256,12]{0,1:T(8,128)S(1)}, f32[256,12]{0,1:T(8,128)S(1)}, u32[]{:S(2)}, u32[]{:S(2)}) collective-permute-start(f32[256,12]{0,1:T(8,128)S(1)} %maximum_bitcast_fusion), channel_id=1, source_target_pairs={{0,1},{1,2},{2,3},{3,0},{4,5},{5,6},{6,7},{7,4},{8,9},{9,10},{10,1... | collective-permute-start | bytes 36872 | tf_op jit(solution)/shard_map/ppermute | solution.py:266
  25.8 2.6 copy-start
  233.0 0.6 copy-start.1
  233.1 0.6 copy-start.2
  255.5 11.9 %collective-permute-start.6 = (f32[256,12]{1,0:T(8,128)S(1)}, f32[256,12]{1,0:T(8,128)S(1)}, u32[]{:S(2)}, u32[]{:S(2)}) collective-permute-start(f32[256,12]{1,0:T(8,128)S(1)} %get-tuple-element.29), channel_id=1, source_target_pairs={{0,1},{1,2},{2,3},{3,0},{4,5},{5,6},{6,7},{7,4},{8,9},{9,10},{10,1... | collective-permute-start | bytes 36872 | tf_op jit(solution)/shard_map/ppermute | solution.py:266
  261.8 8.9 %collective-permute-start.7 = (f32[256,12]{1,0:T(8,128)S(1)}, f32[256,12]{1,0:T(8,128)S(1)}, u32[]{:S(2)}, u32[]{:S(2)}) collective-permute-start(f32[256,12]{1,0:T(8,128)S(1)} %get-tuple-element.30), channel_id=1, source_target_pairs={{1,0},{2,1},{3,2},{0,3},{5,4},{6,5},{7,6},{4,7},{9,8},{10,9},{11,1... | collective-permute-start | bytes 36872 | tf_op jit(solution)/shard_map/ppermute | solution.py:266
  263.6 7.8 %collective-permute-start.4 = (f32[3,4,512]{2,1,0:T(4,128)}, f32[3,4,512]{2,1,0:T(4,128)S(1)}, u32[]{:S(2)}, u32[]{:S(2)}) collective-permute-start(f32[3,4,512]{2,1,0:T(4,128)} %get-tuple-element.7), channel_id=1, source_target_pairs={{0,4},{4,8},{8,12},{12,16},{16,20},{20,24},{24,28},{28,0},{1,5},{5... | collective-permute-start | bytes 73736 | tf_op jit(solution)/shard_map/ppermute | solution.py:266
  264.5 6.9 %collective-permute-start.5 = (f32[3,4,512]{2,1,0:T(4,128)}, f32[3,4,512]{2,1,0:T(4,128)S(1)}, u32[]{:S(2)}, u32[]{:S(2)}) collective-permute-start(f32[3,4,512]{2,1,0:T(4,128)} %get-tuple-element.8), channel_id=1, source_target_pairs={{4,0},{8,4},{12,8},{16,12},{20,16},{24,20},{28,24},{0,28},{5,1},{9... | collective-permute-start | bytes 73736 | tf_op jit(solution)/shard_map/ppermute | solution.py:266
  271.4 0.6 copy-start.3
  271.5 0.6 copy-start.4

commit v3 on v2

--- a/solution.py
+++ b/solution.py
@@ -111,19 +111,21 @@
             o_ref[s, z] = held[z, pl.ds(s * rows, rows), :]
 
 
-def dip_response(scale, x_ref, tw_ref, table_ref, now_ref, past_ref, o_ref, held):
-    count, _, rows, _ = x_ref.shape
-    for l in range(count):
-        real_part = imag_part = None
-        for j in range(count):
-            cos, sin = root(l * j, count)
-            real_part = add_term(real_part, cos, x_ref[j, 0])
-            real_part = add_term(real_part, sin, x_ref[j, 1])
-            imag_part = add_term(imag_part, cos, x_ref[j, 1])
-            imag_part = add_term(imag_part, -sin, x_ref[j, 0])
-        cos, sin = tw_ref[0, l : l + 1, :], tw_ref[1, l : l + 1, :]
-        held[0, pl.ds(l * rows, rows), :] = real_part * cos + imag_part * sin
-        held[1, pl.ds(l * rows, rows), :] = imag_part * cos - real_part * sin
+def dip_response(scale, x_refs, tw_ref, table_ref, now_ref, past_ref, o_refs, held):
+    count, _, rows, width = x_refs[0].shape
+    for h, x_ref in enumerate(x_refs):
+        part = slice(h * width, (h + 1) * width)
+        for l in range(count):
+            real_part = imag_part = None
+            for j in range(count):
+                cos, sin = root(l * j, count)
+                real_part = add_term(real_part, cos, x_ref[j, 0])
+                real_part = add_term(real_part, sin, x_ref[j, 1])
+                imag_part = add_term(imag_part, cos, x_ref[j, 1])
+                imag_part = add_term(imag_part, -sin, x_ref[j, 0])
+            cos, sin = tw_ref[0, l : l + 1, part], tw_ref[1, l : l + 1, part]
+            held[0, pl.ds(l * rows, rows), part] = real_part * cos + imag_part * sin
+            held[1, pl.ds(l * rows, rows), part] = imag_part * cos - real_part * sin
     real_part, imag_part = complex_product(held[0], held[1], table_ref, -1.0, False)
     weight = scale * now_ref[...]
     real_part = weight * real_part + past_ref[0]
@@ -137,18 +139,20 @@
         imag_part = held[1, pl.ds(l * rows, rows), :]
         held[0, pl.ds(l * rows, rows), :] = real_part * cos - imag_part * sin
         held[1, pl.ds(l * rows, rows), :] = imag_part * cos + real_part * sin
-    for j in range(count):
-        real_part = imag_part = None
-        for l in range(count):
-            cos, sin = root(l * j, count)
-            lr = held[0, pl.ds(l * rows, rows), :]
-            li = held[1, pl.ds(l * rows, rows), :]
-            real_part = add_term(real_part, cos, lr)
-            real_part = add_term(real_part, -sin, li)
-            imag_part = add_term(imag_part, cos, li)
-            imag_part = add_term(imag_part, sin, lr)
-        o_ref[j, 0] = real_part
-        o_ref[j, 1] = imag_part
+    for h, o_ref in enumerate(o_refs):
+        part = slice(h * width, (h + 1) * width)
+        for j in range(count):
+            real_part = imag_part = None
+            for l in range(count):
+                cos, sin = root(l * j, count)
+                lr = held[0, pl.ds(l * rows, rows), part]
+                li = held[1, pl.ds(l * rows, rows), part]
+                real_part = add_term(real_part, cos, lr)
+                real_part = add_term(real_part, -sin, li)
+                imag_part = add_term(imag_part, cos, li)
+                imag_part = add_term(imag_part, sin, lr)
+            o_ref[j, 0] = real_part
+            o_ref[j, 1] = imag_part
 
 
 def rows_diff(value, before, after):
@@ -287,6 +291,7 @@
     w2,
     y1,
     held,
+    held_part,
     send_sem,
     recv_sem,
 ):
@@ -352,46 +357,95 @@
         ("bx", y1, o_ref),
     )
 
+    parts = count // past_ref.shape[0]
+
+    def go(stage, g):
+        axis, source, landing = stages[stage]
+        send(stage, axis, g, source, landing)
+
+    def take(stage, g):
+        axis, source, landing = stages[stage]
+        receive(stage, axis, g, source, landing)
+
+    def enter(g):
+        take(0, g)
+        strike_forward(sizes["bx"], x1.at[g], b1.at[g])
+        go(1, g)
+
+    def across(g):
+        take(1, g)
+        strike_cells_dft(-1.0, b2.at[g], strike_tw_ref, strike_table_ref, t1.at[g], held_part)
+        go(2, g)
+
+    def back(g):
+        take(3, g)
+        strike_cells_dft(1.0, u2.at[g], strike_tw_ref, strike_table_ref, w1.at[g], held_part)
+        go(4, g)
+
+    def leave(g):
+        take(4, g)
+        strike_inverse(sizes["bx"], scale, w2.at[g], y1.at[g])
+        go(5, g)
+
+    go(0, 0)
+    go(0, 1)
+    enter(0)
+
+    @pl.loop(0, count - 1)
+    def _(g):
+        @pl.when(g + 2 < count)
+        def _():
+            go(0, g + 2)
+
+        enter(g + 1)
+        across(g)
+
+    across(count - 1)
+
+    @pl.loop(0, past_ref.shape[0])
+    def _(c):
+        for h in range(parts):
+            take(2, c * parts + h)
+        dip_response(
+            scale,
+            [t2.at[c * parts + h] for h in range(parts)],
+            dip_tw_ref,
+            dip_table_ref,
+            now_ref,
+            past_ref.at[c],
+            [u1.at[c * parts + h] for h in range(parts)],
+            held,
+        )
+        for h in range(parts):
+            go(3, c * parts + h)
+
+    back(0)
+
+    @pl.loop(1, count)
+    def _(g):
+        back(g)
+        leave(g - 1)
+
+    leave(count - 1)
+
     @pl.loop(0, count)
-    def _(c):
-        send(0, stages[0][0], c, *stages[0][1:])
-
-    def work(stage, c):
-        if stage == 0:
-            strike_forward(sizes["bx"], x1.at[c], b1.at[c])
-        elif stage == 1:
-            strike_cells_dft(-1.0, b2.at[c], strike_tw_ref, strike_table_ref, t1.at[c], held)
-        elif stage == 2:
-            dip_response(
-                scale, t2.at[c], dip_tw_ref, dip_table_ref, now_ref, past_ref.at[c], u1.at[c], held
-            )
-        elif stage == 3:
-            strike_cells_dft(1.0, u2.at[c], strike_tw_ref, strike_table_ref, w1.at[c], held)
-        else:
-            strike_inverse(sizes["bx"], scale, w2.at[c], y1.at[c])
-
-    for stage in range(5):
-
-        @pl.loop(0, count)
-        def _(c):
-            receive(stage, stages[stage][0], c, *stages[stage][1:])
-            work(stage, c)
-            send(stage + 1, stages[stage + 1][0], c, *stages[stage + 1][1:])
-
-    @pl.loop(0, count)
-    def _(c):
-        receive(5, stages[5][0], c, *stages[5][1:])
+    def _(g):
+        take(5, g)
 
 
 def fault_traction(interface, now, past, tables, scale):
     strike_count, dip_count = lax.axis_size("bx"), lax.axis_size("by")
     count, cells, width = interface.shape
     rows, modes = cells // strike_count, cells // dip_count
-    flat = (count, strike_count, rows, width)
-    wide = (count, strike_count, 2, rows, width)
-    tall = (count, dip_count, 2, modes, width)
+    parts = 2 if width % 256 == 0 else 1
+    narrow = width // parts
+    face = interface.reshape(count, strike_count, rows, parts, narrow).transpose(0, 3, 1, 2, 4)
+    chunks = count * parts
+    flat = (chunks, strike_count, rows, narrow)
+    wide = (chunks, strike_count, 2, rows, narrow)
+    tall = (chunks, dip_count, 2, modes, narrow)
     peers = max(strike_count, dip_count)
-    operands = (interface.reshape(flat), *tables, now, past)
+    operands = (face.reshape(flat), *tables, now, past)
     out = pl.pallas_call(
         partial(fault_kernel, scale),
         out_shape=struct(flat),
@@ -401,14 +455,16 @@
             *[pltpu.VMEM(s, F32) for s in (flat, wide, wide, tall, tall, tall, tall, wide, wide)],
             pltpu.VMEM(flat, F32),
             pltpu.VMEM((2, cells, width), F32),
-            pltpu.SemaphoreType.DMA((6, count, peers)),
-            pltpu.SemaphoreType.DMA((6, count, peers)),
+            pltpu.VMEM((2, cells, narrow), F32),
+            pltpu.SemaphoreType.DMA((6, chunks, peers)),
+            pltpu.SemaphoreType.DMA((6, chunks, peers)),
         ],
         compiler_params=pltpu.CompilerParams(
             collective_id=0, has_side_effects=True, vmem_limit_bytes=60 * 1024 * 1024
         ),
         name="fault_traction",
     )(*operands)
+    out = out.reshape(count, parts, cells, narrow).transpose(0, 2, 1, 3)
     return out.reshape(count, cells, width)
 
 

time: 290 us -> 280 us (0.966)
  Pallas kernels: 241 us -> 221 us
  local copies, waits for them, and re-layouts: 15.7 us -> 27.1 us
    pallas_call x1, Pallas kernels: 203 us -> 182 us  [fault_traction(): pl.pallas_call(partial(fault_kernel, scale), out_shape=struct(flat), in_s...]
    reshape x0 -> x4, local copies, waits for them, and re-layouts: none -> 10.8 us  [the longest x2 5.82 us: fault_traction(): interface.reshape(count, strike_count, rows, parts, narrow)]
  transfers between devices with their start and end apart: 8 -> 8, of which waited for: 2 -> 2; matrix products, arithmetic and copies ran while one was open for 7% -> 11% of each run, Pallas kernels for 70% -> 65%
where the time goes in v3:
time: 280 us
  Pallas kernels  221 us (79%)
  local copies, waits for them, and re-layouts  27.1 us (10%)
  starting transfers between devices  18.4 us (7%)
  other arithmetic  8.77 us (3%)
  waiting for transfers between devices  4.23 us (2%)
    pallas_call x1, Pallas kernels, fault_traction(): pl.pallas_call(partial(fault_kernel, scale), out_shape=struct(flat), in_s...  182 us
    pallas_call x1, Pallas kernels, local(): pl.pallas_call(velocity_step, grid=grid, in_specs=[tile_spec(stress.shape...  20.8 us
    pallas_call x1, Pallas kernels, local(): pl.pallas_call(stress_step, grid=grid, in_specs=[tile_spec(velocity.shape...  17.5 us
    ppermute x4, starting transfers between devices, edges(): lax.ppermute(first, axis, backward)  11.3 us
    transpose x1, other arithmetic, local(): past = past.reshape(2, 3, modes, dip_count, width).transpose(1, 0, 3, 2, 4)  7.91 us
    ppermute x4, starting transfers between devices, edges(): lax.ppermute(last, axis, forward)  7.09 us
    reshape x2, local copies, waits for them, and re-layouts, fault_traction(): interface.reshape(count, strike_count, rows, parts, narrow)  5.82 us
  transfers between devices with their start and end apart: 8, of which 2 were waited for; matrix products, arithmetic and copies ran while one was open for 11% of the time, Pallas kernels for 65%

profile of v3, /device:TPU:0, one launch (start us, length us, event | category | flops | bytes accessed | tf_op | source)
XLA Modules:
  0.0 280.1 jit_solution(1140207238232573332)
XLA Ops:
  0.6 1.0 fusion.14
  1.7 0.5 collective-permute-start
  2.3 2.9 %collective-permute-start.1 = (f32[3,4,512]{2,1,0:T(4,128)S(1)}, f32[3,4,512]{2,1,0:T(4,128)S(1)}, u32[]{:S(2)}, u32[]{:S(2)}) collective-permute-start(f32[3,4,512]{2,1,0:T(4,128)S(1)} %pad_maximum_fusion.2), channel_id=1, source_target_pairs={{4,0},{8,4},{12,8},{16,12},{20,16},{24,20},{28,24},{0,28},{5,1},{9... | collective-permute-start | bytes 73736 | tf_op jit(solution)/shard_map/ppermute | solution.py:270
  5.2 2.4 fusion.13
  7.8 0.2 copy.92
  8.0 0.2 copy.91
  8.3 4.4 %collective-permute-start.3 = (f32[256,12]{0,1:T(8,128)S(1)}, f32[256,12]{0,1:T(8,128)S(1)}, u32[]{:S(2)}, u32[]{:S(2)}) collective-permute-start(f32[256,12]{0,1:T(8,128)S(1)} %maximum_bitcast_fusion.1), channel_id=1, source_target_pairs={{1,0},{2,1},{3,2},{0,3},{5,4},{6,5},{7,6},{4,7},{9,8},{10,9},{11,1... | collective-permute-start | bytes 36872 | tf_op jit(solution)/shard_map/ppermute | solution.py:270
  12.8 0.2 copy.89
  13.0 0.2 copy.88
  13.4 3.6 %slice_bitcast_fusion.10 = (f32[64,4,512]{2,1,0:T(4,128)S(1)}, f32[64,4,512]{2,1,0:T(4,128)S(1)}, f32[64,4,512]{2,1,0:T(4,128)S(1)}, f32[64,4,512]{2,1,0:T(4,128...) fusion(f32[7,64,1,4,512]{4,3,2,1,0:T(4,128)} %param.11), kind=kLoop, calls=%fused_computation.23 | loop fusion | bytes 7340032 | tf_op jit(solution)/shard_map/mul | solution.py:500
  17.0 7.9 %fusion.2 = f32[3,2,4,64,512]{4,2,3,0,1:T(4,128)S(1)} fusion(f32[6,2,3,64,1,4,512]{6,5,3,2,1,4,0:T(4,128)} %bitcast.96, f32[6,2,3,64,1,4,512]{6,5,4,3,2,1,0:T(4,128)} %param.10, f32[64,4,512]{2,1,0:T(4,128)S(1)} %get-tuple-element.27, f32[64,4,512]{2,1,0:T(4,128)S(1)} %get-tuple-element.28, f32[64,4,512]{2,1,0:T(4,128)S(1)} %get-tuple-element.23, ...), kind=kLoop, calls=%fused_computation.3 | loop fusion | flops 8650752 | bytes 25165824 | tf_op jit(solution)/shard_map/transpose | solution.py:504
  24.9 0.8 copy.78.strike_tw_ref
  25.7 3.0 %reshape.90 = f32[3,8,32,2,256]{4,3,2,1,0:T(2,128)} reshape(f32[3,256,512]{2,1,0:T(8,128)} %w_ref.1) | data formatting | bytes 3145728 | tf_op jit(solution)/shard_map/reshape | solution.py:442
  28.8 2.8 copy.70
  31.6 2.6 copy.77
  34.2 1.0 copy.71
  35.2 182.5 %fault_traction.1 = f32[6,8,32,256]{3,2,1,0:T(8,128)} custom-call(f32[6,8,32,256]{3,2,1,0:T(8,128)} %bitcast.98, f32[256,2]{1,0:T(8,128)} %copy.78.strike_tw_ref, bf16[2,2,256,256]{3,2,1,0:T(8,128)(2,1)} %constant.15.clone.strike_table_ref, f32[2,4,512]{2,1,0:T(4,128)} %constant.14.clone.dip_tw_ref, bf16[2,2,512,512]{3,2,1,0:T(8,128)(2,1)} %constant.16.clone.dip_table_ref, ...), custom_call_target="tpu_custom_call" | custom-call | tf_op jit(solution)/shard_map/fault_traction/pallas_call | solution.py:449
  217.7 2.6 copy.100
  220.3 2.4 reshape.95.t_ref
  222.7 0.7 copy.80.col_ref
  223.5 0.6 copy-done.1
  224.1 0.6 copy-done.2
  224.7 20.8 %velocity_step.1 = (f32[3,4,256,512]{3,2,1,0:T(8,128)}, f32[256,24]{1,0:T(8,128)}, f32[3,4,512]{2,1,0:T(4,128)}, f32[3,4,512]{2,1,0:T(4,128)}) custom-call(f32[6,4,256,512]{3,2,1,0:T(8,128)} %s_ref.3, f32[6,4,256,512]{3,2,1,0:T(8,128)} %s_ref.3, f32[6,4,256,512]{3,2,1,0:T(8,128)} %s_ref.3, f32[3,4,512]{2,1,0:T(4,128)} %copy-done.1, f32[3,4,512]{2,1,0:T(4,128)} %copy-done.2, ...), custom_call_target="tpu_custom_call" | custom-call | flops 10000000 | bytes 25165824 | tf_op jit(solution)/shard_map/velocity_step/pallas_call | solution.py:527
  245.5 1.1 fusion.15
  246.5 6.3 %collective-permute-start.6 = (f32[256,12]{1,0:T(8,128)S(1)}, f32[256,12]{1,0:T(8,128)S(1)}, u32[]{:S(2)}, u32[]{:S(2)}) collective-permute-start(f32[256,12]{1,0:T(8,128)S(1)} %get-tuple-element.29), channel_id=1, source_target_pairs={{0,1},{1,2},{2,3},{3,0},{4,5},{5,6},{6,7},{7,4},{8,9},{9,10},{10,1... | collective-permute-start | bytes 36872 | tf_op jit(solution)/shard_map/ppermute | solution.py:270
  252.9 1.5 collective-permute-start.7
  254.5 2.5 collective-permute-start.5
  257.0 1.7 collective-permute-done.6
  258.7 2.5 collective-permute-done.7
  261.2 0.8 pad_maximum_fusion.col_ref
  262.0 0.6 copy-done.3
  262.6 17.5 %stress_step.1 = f32[6,4,256,512]{3,2,1,0:T(8,128)} custom-call(f32[3,4,256,512]{3,2,1,0:T(8,128)} %get-tuple-element.4.v_ref.prev_ref.next_ref, f32[3,4,256,512]{3,2,1,0:T(8,128)} %get-tuple-element.4.v_ref.prev_ref.next_ref, f32[3,4,256,512]{3,2,1,0:T(8,128)} %get-tuple-element.4.v_ref.prev_ref.next_ref, f32[3,4,512]{2,1,0:T(4,128)} %copy-done.3, ...), custom_call_target="tpu_custom_call" | custom-call | flops 20000000 | bytes 31457280 | tf_op jit(solution)/shard_map/stress_step/pallas_call | solution.py:552
  (28 shorter events, 0.8 us)
Async XLA Ops:
  1.7 221.7 %collective-permute-start = (f32[3,4,512]{2,1,0:T(4,128)S(1)}, f32[3,4,512]{2,1,0:T(4,128)S(1)}, u32[]{:S(2)}, u32[]{:S(2)}) collective-permute-start(f32[3,4,512]{2,1,0:T(4,128)S(1)} %pad_maximum_fusion.1), channel_id=1, source_target_pairs={{0,4},{4,8},{8,12},{12,16},{16,20},{20,24},{24,28},{28,0},{1,5},{5... | collective-permute-start | bytes 73736 | tf_op jit(solution)/shard_map/ppermute | solution.py:270
  2.3 221.2 %collective-permute-start.1 = (f32[3,4,512]{2,1,0:T(4,128)S(1)}, f32[3,4,512]{2,1,0:T(4,128)S(1)}, u32[]{:S(2)}, u32[]{:S(2)}) collective-permute-start(f32[3,4,512]{2,1,0:T(4,128)S(1)} %pad_maximum_fusion.2), channel_id=1, source_target_pairs={{4,0},{8,4},{12,8},{16,12},{20,16},{24,20},{28,24},{0,28},{5,1},{9... | collective-permute-start | bytes 73736 | tf_op jit(solution)/shard_map/ppermute | solution.py:270
  8.3 214.4 %collective-permute-start.3 = (f32[256,12]{0,1:T(8,128)S(1)}, f32[256,12]{0,1:T(8,128)S(1)}, u32[]{:S(2)}, u32[]{:S(2)}) collective-permute-start(f32[256,12]{0,1:T(8,128)S(1)} %maximum_bitcast_fusion.1), channel_id=1, source_target_pairs={{1,0},{2,1},{3,2},{0,3},{5,4},{6,5},{7,6},{4,7},{9,8},{10,9},{11,1... | collective-permute-start | bytes 36872 | tf_op jit(solution)/shard_map/ppermute | solution.py:270
  13.2 209.5 %collective-permute-start.2 = (f32[256,12]{0,1:T(8,128)S(1)}, f32[256,12]{0,1:T(8,128)S(1)}, u32[]{:S(2)}, u32[]{:S(2)}) collective-permute-start(f32[256,12]{0,1:T(8,128)S(1)} %maximum_bitcast_fusion), channel_id=1, source_target_pairs={{0,1},{1,2},{2,3},{3,0},{4,5},{5,6},{6,7},{7,4},{8,9},{9,10},{10,1... | collective-permute-start | bytes 36872 | tf_op jit(solution)/shard_map/ppermute | solution.py:270
  31.6 2.6 copy-start
  223.5 0.6 copy-start.1
  224.1 0.6 copy-start.2
  246.5 12.1 %collective-permute-start.6 = (f32[256,12]{1,0:T(8,128)S(1)}, f32[256,12]{1,0:T(8,128)S(1)}, u32[]{:S(2)}, u32[]{:S(2)}) collective-permute-start(f32[256,12]{1,0:T(8,128)S(1)} %get-tuple-element.29), channel_id=1, source_target_pairs={{0,1},{1,2},{2,3},{3,0},{4,5},{5,6},{6,7},{7,4},{8,9},{9,10},{10,1... | collective-permute-start | bytes 36872 | tf_op jit(solution)/shard_map/ppermute | solution.py:270
  252.9 8.4 %collective-permute-start.7 = (f32[256,12]{1,0:T(8,128)S(1)}, f32[256,12]{1,0:T(8,128)S(1)}, u32[]{:S(2)}, u32[]{:S(2)}) collective-permute-start(f32[256,12]{1,0:T(8,128)S(1)} %get-tuple-element.30), channel_id=1, source_target_pairs={{1,0},{2,1},{3,2},{0,3},{5,4},{6,5},{7,6},{4,7},{9,8},{10,9},{11,1... | collective-permute-start | bytes 36872 | tf_op jit(solution)/shard_map/ppermute | solution.py:270
  254.4 7.6 %collective-permute-start.4 = (f32[3,4,512]{2,1,0:T(4,128)}, f32[3,4,512]{2,1,0:T(4,128)S(1)}, u32[]{:S(2)}, u32[]{:S(2)}) collective-permute-start(f32[3,4,512]{2,1,0:T(4,128)} %get-tuple-element.7), channel_id=1, source_target_pairs={{0,4},{4,8},{8,12},{12,16},{16,20},{20,24},{24,28},{28,0},{1,5},{5... | collective-permute-start | bytes 73736 | tf_op jit(solution)/shard_map/ppermute | solution.py:270
  254.5 7.4 %collective-permute-start.5 = (f32[3,4,512]{2,1,0:T(4,128)}, f32[3,4,512]{2,1,0:T(4,128)S(1)}, u32[]{:S(2)}, u32[]{:S(2)}) collective-permute-start(f32[3,4,512]{2,1,0:T(4,128)} %get-tuple-element.8), channel_id=1, source_target_pairs={{4,0},{8,4},{12,8},{16,12},{20,16},{24,20},{28,24},{0,28},{5,1},{9... | collective-permute-start | bytes 73736 | tf_op jit(solution)/shard_map/ppermute | solution.py:270
  262.0 0.6 copy-start.3
  262.0 0.6 copy-start.4

commit v4 on v3

--- a/solution.py
+++ b/solution.py
@@ -295,7 +295,8 @@
     send_sem,
     recv_sem,
 ):
-    count = face_ref.shape[0]
+    count, narrow = x1.shape[0], x1.shape[-1]
+    parts = count // past_ref.shape[0]
     sizes = {"bx": lax.axis_size("bx"), "by": lax.axis_size("by")}
     place = {"bx": lax.axis_index("bx"), "by": lax.axis_index("by")}
 
@@ -316,12 +317,19 @@
 
     pl.semaphore_wait(barrier, sizes["bx"] + sizes["by"] - 2)
 
+    def piece(ref, g, slot):
+        if len(ref.shape) == 4 and ref.shape[0] != count:
+            return ref.at[g // parts, slot, :, pl.ds(pl.multiple_of(g % parts * narrow, narrow), narrow)]
+        if ref is face_ref or ref is o_ref:
+            return ref.at[g, slot, :, pl.ds(0, narrow)]
+        return ref.at[g, slot]
+
     def copy(stage, axis, c, k, source, landing):
         me = place[axis]
         target = lax.rem(me + k, sizes[axis])
         return pltpu.make_async_remote_copy(
-            src_ref=source.at[c, target],
-            dst_ref=landing.at[c, me],
+            src_ref=piece(source, c, target),
+            dst_ref=piece(landing, c, me),
             send_sem=send_sem.at[stage, c, k],
             recv_sem=recv_sem.at[stage, c, k],
             device_id=device(axis, target),
@@ -331,7 +339,7 @@
     def own(stage, axis, c, source, landing):
         me = place[axis]
         return pltpu.make_async_copy(
-            source.at[c, me], landing.at[c, me], recv_sem.at[stage, c, 0]
+            piece(source, c, me), piece(landing, c, me), recv_sem.at[stage, c, 0]
         )
 
     def send(stage, axis, c, source, landing):
@@ -357,8 +365,6 @@
         ("bx", y1, o_ref),
     )
 
-    parts = count // past_ref.shape[0]
-
     def go(stage, g):
         axis, source, landing = stages[stage]
         send(stage, axis, g, source, landing)
@@ -389,18 +395,20 @@
 
     go(0, 0)
     go(0, 1)
-    enter(0)
-
-    @pl.loop(0, count - 1)
+
+    @pl.loop(0, count + 1)
     def _(g):
+        @pl.when(g < count)
+        def _():
+            enter(g)
+
         @pl.when(g + 2 < count)
         def _():
             go(0, g + 2)
 
-        enter(g + 1)
-        across(g)
-
-    across(count - 1)
+        @pl.when(g > 0)
+        def _():
+            across(g - 1)
 
     @pl.loop(0, past_ref.shape[0])
     def _(c):
@@ -419,14 +427,15 @@
         for h in range(parts):
             go(3, c * parts + h)
 
-    back(0)
-
-    @pl.loop(1, count)
+    @pl.loop(0, count + 1)
     def _(g):
-        back(g)
-        leave(g - 1)
-
-    leave(count - 1)
+        @pl.when(g < count)
+        def _():
+            back(g)
+
+        @pl.when(g > 0)
+        def _():
+            leave(g - 1)
 
     @pl.loop(0, count)
     def _(g):
@@ -439,16 +448,16 @@
     rows, modes = cells // strike_count, cells // dip_count
     parts = 2 if width % 256 == 0 else 1
     narrow = width // parts
-    face = interface.reshape(count, strike_count, rows, parts, narrow).transpose(0, 3, 1, 2, 4)
+    face = interface.reshape(count, strike_count, rows, width)
     chunks = count * parts
     flat = (chunks, strike_count, rows, narrow)
     wide = (chunks, strike_count, 2, rows, narrow)
     tall = (chunks, dip_count, 2, modes, narrow)
     peers = max(strike_count, dip_count)
-    operands = (face.reshape(flat), *tables, now, past)
+    operands = (face, *tables, now, past)
     out = pl.pallas_call(
         partial(fault_kernel, scale),
-        out_shape=struct(flat),
+        out_shape=struct(face.shape),
         in_specs=[pl.BlockSpec(memory_space=pltpu.VMEM)] * len(operands),
         out_specs=pl.BlockSpec(memory_space=pltpu.VMEM),
         scratch_shapes=[
@@ -464,7 +473,6 @@
         ),
         name="fault_traction",
     )(*operands)
-    out = out.reshape(count, parts, cells, narrow).transpose(0, 2, 1, 3)
     return out.reshape(count, cells, width)
 
 
@@ -495,7 +503,12 @@
     strike_tw = jnp.stack([jnp.cos(angle), jnp.sin(angle)], axis=1)
     lane = np.outer(np.arange(dip_count), np.arange(width)) * (2.0 * math.pi / dip_length)
     dip_tw = jnp.asarray(np.stack([np.cos(lane), np.sin(lane)]).astype(np.float32))
-    tables = (strike_tw, square_table(cells), dip_tw, square_table(width))
+    dip_table = lax.optimization_barrier(square_table(width))
+    if width % cells == 0:
+        strike_table = dip_table[:, :, :: width // cells, :cells]
+    else:
+        strike_table = square_table(cells)
+    tables = (strike_tw, strike_table, dip_tw, dip_table)
 
     past = kernel[1] * history[0]
     for h in range(1, history.shape[0]):

time: 280 us -> 276 us (0.986)
  local copies, waits for them, and re-layouts: 27.1 us -> 22.8 us
    reshape x4 -> x0, local copies, waits for them, and re-layouts: 10.8 us -> none  [the longest x2 5.82 us: fault_traction(): interface.reshape(count, strike_count, rows, parts, narrow)]
    slice x0 -> x1, local copies, waits for them, and re-layouts: none -> 7.12 us  [local(): strike_table = dip_table[:, :, ::width // cells, :cells]]
  transfers between devices with their start and end apart: 8 -> 8, of which waited for: 2 -> 2; matrix products, arithmetic and copies ran while one was open for 11% -> 10% of each run, Pallas kernels for 65% -> 66%
where the time goes in v4:
time: 276 us
  Pallas kernels  221 us (80%)
  local copies, waits for them, and re-layouts  22.8 us (8%)
  starting transfers between devices  18.4 us (7%)
  other arithmetic  8.78 us (3%)
  waiting for transfers between devices  4.24 us (2%)
    pallas_call x1, Pallas kernels, fault_traction(): pl.pallas_call(partial(fault_kernel, scale), out_shape=struct(face.shape)...  182 us
    pallas_call x1, Pallas kernels, local(): pl.pallas_call(velocity_step, grid=grid, in_specs=[tile_spec(stress.shape...  20.8 us
    pallas_call x1, Pallas kernels, local(): pl.pallas_call(stress_step, grid=grid, in_specs=[tile_spec(velocity.shape...  17.5 us
    ppermute x4, starting transfers between devices, edges(): lax.ppermute(first, axis, backward)  11.3 us
    transpose x1, other arithmetic, local(): past = past.reshape(2, 3, modes, dip_count, width).transpose(1, 0, 3, 2, 4)  7.91 us
    slice x1, local copies, waits for them, and re-layouts, local(): strike_table = dip_table[:, :, ::width // cells, :cells]  7.12 us
    ppermute x4, starting transfers between devices, edges(): lax.ppermute(last, axis, forward)  7.11 us
  transfers between devices with their start and end apart: 8, of which 2 were waited for; matrix products, arithmetic and copies ran while one was open for 10% of the time, Pallas kernels for 66%

profile of v4, /device:TPU:0, one launch (start us, length us, event | category | flops | bytes accessed | tf_op | source)
XLA Modules:
  0.0 275.8 jit_solution(10951714385067809872)
XLA Ops:
  0.6 1.0 fusion.14
  1.7 0.5 collective-permute-start
  2.3 2.9 %collective-permute-start.1 = (f32[3,4,512]{2,1,0:T(4,128)S(1)}, f32[3,4,512]{2,1,0:T(4,128)S(1)}, u32[]{:S(2)}, u32[]{:S(2)}) collective-permute-start(f32[3,4,512]{2,1,0:T(4,128)S(1)} %pad_maximum_fusion.2), channel_id=1, source_target_pairs={{4,0},{8,4},{12,8},{16,12},{20,16},{24,20},{28,24},{0,28},{5,1},{9... | collective-permute-start | bytes 73736 | tf_op jit(solution)/shard_map/ppermute | solution.py:270
  5.2 2.4 fusion.13
  7.7 0.2 copy.83
  7.8 0.2 copy.85
  8.0 0.2 copy.84
  8.3 4.4 %collective-permute-start.3 = (f32[256,12]{0,1:T(8,128)S(1)}, f32[256,12]{0,1:T(8,128)S(1)}, u32[]{:S(2)}, u32[]{:S(2)}) collective-permute-start(f32[256,12]{0,1:T(8,128)S(1)} %maximum_bitcast_fusion.1), channel_id=1, source_target_pairs={{1,0},{2,1},{3,2},{0,3},{5,4},{6,5},{7,6},{4,7},{9,8},{10,9},{11,1... | collective-permute-start | bytes 36872 | tf_op jit(solution)/shard_map/ppermute | solution.py:270
  12.6 0.2 copy.80
  12.8 0.2 copy.82
  13.0 0.2 copy.81
  13.2 0.1 collective-permute-start.2
  13.4 3.6 %slice_bitcast_fusion.10 = (f32[64,4,512]{2,1,0:T(4,128)S(1)}, f32[64,4,512]{2,1,0:T(4,128)S(1)}, f32[64,4,512]{2,1,0:T(4,128)S(1)}, f32[64,4,512]{2,1,0:T(4,128...) fusion(f32[7,64,1,4,512]{4,3,2,1,0:T(4,128)} %param.10), kind=kLoop, calls=%fused_computation.22 | loop fusion | bytes 7340032 | tf_op jit(solution)/shard_map/mul | solution.py:513
  17.0 7.9 %fusion.2 = f32[3,2,4,64,512]{4,2,3,0,1:T(4,128)S(1)} fusion(f32[6,2,3,64,1,4,512]{6,5,3,2,1,4,0:T(4,128)} %bitcast.91, f32[6,2,3,64,1,4,512]{6,5,4,3,2,1,0:T(4,128)} %param.9, f32[64,4,512]{2,1,0:T(4,128)S(1)} %get-tuple-element.27, f32[64,4,512]{2,1,0:T(4,128)S(1)} %get-tuple-element.28, f32[64,4,512]{2,1,0:T(4,128)S(1)} %get-tuple-element.23, ...), kind=kLoop, calls=%fused_computation.3 | loop fusion | flops 8650752 | bytes 25165824 | tf_op jit(solution)/shard_map/transpose | solution.py:517
  24.9 0.8 copy.72.strike_tw_ref
  25.7 7.1 %slice.96.strike_table_ref = bf16[2,2,256,256]{3,2,1,0:T(8,128)(2,1)} slice(bf16[2,2,512,512]{3,2,1,0:T(8,128)(2,1)} %constant.13.clone.dip_table_ref), slice={[0:2:1], [0:2:1], [0:512:2], [0:256:1]} | slice | bytes 1048576 | tf_op jit(solution)/shard_map/slice | solution.py:508
  32.9 2.6 copy.71
  35.5 1.0 copy.65
  36.5 182.5 %fault_traction.1 = f32[3,8,32,512]{3,2,1,0:T(8,128)} custom-call(f32[3,8,32,512]{3,2,1,0:T(8,128)} %bitcast.93, f32[256,2]{1,0:T(8,128)} %copy.72.strike_tw_ref, bf16[2,2,256,256]{3,2,1,0:T(8,128)(2,1)} %slice.96.strike_table_ref, f32[2,4,512]{2,1,0:T(4,128)} %constant.12.clone.dip_tw_ref, bf16[2,2,512,512]{3,2,1,0:T(8,128)(2,1)} %constant.13.clone.dip_table_ref, ...), custom_call_target="tpu_custom_call" | custom-call | tf_op jit(solution)/shard_map/fault_traction/pallas_call | solution.py:458
  219.0 0.8 copy.73.col_ref
  219.8 0.6 copy-done.1
  220.4 20.8 %velocity_step.1 = (f32[3,4,256,512]{3,2,1,0:T(8,128)}, f32[256,24]{1,0:T(8,128)}, f32[3,4,512]{2,1,0:T(4,128)}, f32[3,4,512]{2,1,0:T(4,128)}) custom-call(f32[6,4,256,512]{3,2,1,0:T(8,128)} %s_ref.3, f32[6,4,256,512]{3,2,1,0:T(8,128)} %s_ref.3, f32[6,4,256,512]{3,2,1,0:T(8,128)} %s_ref.3, f32[3,4,512]{2,1,0:T(4,128)} %copy-done.1, f32[3,4,512]{2,1,0:T(4,128)} %copy-done.2, ...), custom_call_target="tpu_custom_call" | custom-call | flops 10000000 | bytes 25165824 | tf_op jit(solution)/shard_map/velocity_step/pallas_call | solution.py:540
  241.2 1.1 fusion.15
  242.3 6.3 %collective-permute-start.6 = (f32[256,12]{1,0:T(8,128)S(1)}, f32[256,12]{1,0:T(8,128)S(1)}, u32[]{:S(2)}, u32[]{:S(2)}) collective-permute-start(f32[256,12]{1,0:T(8,128)S(1)} %get-tuple-element.29), channel_id=1, source_target_pairs={{0,1},{1,2},{2,3},{3,0},{4,5},{5,6},{6,7},{7,4},{8,9},{9,10},{10,1... | collective-permute-start | bytes 36872 | tf_op jit(solution)/shard_map/ppermute | solution.py:270
  248.6 1.5 collective-permute-start.7
  250.1 0.2 collective-permute-start.4
  250.3 2.5 collective-permute-start.5
  252.7 1.7 collective-permute-done.6
  254.4 2.5 collective-permute-done.7
  257.0 0.8 pad_maximum_fusion.col_ref
  257.7 0.6 copy-done.3
  258.3 17.5 %stress_step.1 = f32[6,4,256,512]{3,2,1,0:T(8,128)} custom-call(f32[3,4,256,512]{3,2,1,0:T(8,128)} %get-tuple-element.4.v_ref.prev_ref.next_ref, f32[3,4,256,512]{3,2,1,0:T(8,128)} %get-tuple-element.4.v_ref.prev_ref.next_ref, f32[3,4,256,512]{3,2,1,0:T(8,128)} %get-tuple-element.4.v_ref.prev_ref.next_ref, f32[3,4,512]{2,1,0:T(4,128)} %copy-done.3, ...), custom_call_target="tpu_custom_call" | custom-call | flops 20000000 | bytes 31457280 | tf_op jit(solution)/shard_map/stress_step/pallas_call | solution.py:565
  (25 shorter events, 0.2 us)
Async XLA Ops:
  1.7 218.0 %collective-permute-start = (f32[3,4,512]{2,1,0:T(4,128)S(1)}, f32[3,4,512]{2,1,0:T(4,128)S(1)}, u32[]{:S(2)}, u32[]{:S(2)}) collective-permute-start(f32[3,4,512]{2,1,0:T(4,128)S(1)} %pad_maximum_fusion.1), channel_id=1, source_target_pairs={{0,4},{4,8},{8,12},{12,16},{16,20},{20,24},{24,28},{28,0},{1,5},{5... | collective-permute-start | bytes 73736 | tf_op jit(solution)/shard_map/ppermute | solution.py:270
  2.3 217.5 %collective-permute-start.1 = (f32[3,4,512]{2,1,0:T(4,128)S(1)}, f32[3,4,512]{2,1,0:T(4,128)S(1)}, u32[]{:S(2)}, u32[]{:S(2)}) collective-permute-start(f32[3,4,512]{2,1,0:T(4,128)S(1)} %pad_maximum_fusion.2), channel_id=1, source_target_pairs={{4,0},{8,4},{12,8},{16,12},{20,16},{24,20},{28,24},{0,28},{5,1},{9... | collective-permute-start | bytes 73736 | tf_op jit(solution)/shard_map/ppermute | solution.py:270
  8.3 210.7 %collective-permute-start.3 = (f32[256,12]{0,1:T(8,128)S(1)}, f32[256,12]{0,1:T(8,128)S(1)}, u32[]{:S(2)}, u32[]{:S(2)}) collective-permute-start(f32[256,12]{0,1:T(8,128)S(1)} %maximum_bitcast_fusion.1), channel_id=1, source_target_pairs={{1,0},{2,1},{3,2},{0,3},{5,4},{6,5},{7,6},{4,7},{9,8},{10,9},{11,1... | collective-permute-start | bytes 36872 | tf_op jit(solution)/shard_map/ppermute | solution.py:270
  13.2 205.7 %collective-permute-start.2 = (f32[256,12]{0,1:T(8,128)S(1)}, f32[256,12]{0,1:T(8,128)S(1)}, u32[]{:S(2)}, u32[]{:S(2)}) collective-permute-start(f32[256,12]{0,1:T(8,128)S(1)} %maximum_bitcast_fusion), channel_id=1, source_target_pairs={{0,1},{1,2},{2,3},{3,0},{4,5},{5,6},{6,7},{7,4},{8,9},{9,10},{10,1... | collective-permute-start | bytes 36872 | tf_op jit(solution)/shard_map/ppermute | solution.py:270
  32.9 2.6 copy-start
  219.8 0.6 copy-start.1
  219.8 0.6 copy-start.2
  242.3 12.2 %collective-permute-start.6 = (f32[256,12]{1,0:T(8,128)S(1)}, f32[256,12]{1,0:T(8,128)S(1)}, u32[]{:S(2)}, u32[]{:S(2)}) collective-permute-start(f32[256,12]{1,0:T(8,128)S(1)} %get-tuple-element.29), channel_id=1, source_target_pairs={{0,1},{1,2},{2,3},{3,0},{4,5},{5,6},{6,7},{7,4},{8,9},{9,10},{10,1... | collective-permute-start | bytes 36872 | tf_op jit(solution)/shard_map/ppermute | solution.py:270
  248.6 8.4 %collective-permute-start.7 = (f32[256,12]{1,0:T(8,128)S(1)}, f32[256,12]{1,0:T(8,128)S(1)}, u32[]{:S(2)}, u32[]{:S(2)}) collective-permute-start(f32[256,12]{1,0:T(8,128)S(1)} %get-tuple-element.30), channel_id=1, source_target_pairs={{1,0},{2,1},{3,2},{0,3},{5,4},{6,5},{7,6},{4,7},{9,8},{10,9},{11,1... | collective-permute-start | bytes 36872 | tf_op jit(solution)/shard_map/ppermute | solution.py:270
  250.1 7.6 %collective-permute-start.4 = (f32[3,4,512]{2,1,0:T(4,128)}, f32[3,4,512]{2,1,0:T(4,128)S(1)}, u32[]{:S(2)}, u32[]{:S(2)}) collective-permute-start(f32[3,4,512]{2,1,0:T(4,128)} %get-tuple-element.7), channel_id=1, source_target_pairs={{0,4},{4,8},{8,12},{12,16},{16,20},{20,24},{24,28},{28,0},{1,5},{5... | collective-permute-start | bytes 73736 | tf_op jit(solution)/shard_map/ppermute | solution.py:270
  250.3 7.4 %collective-permute-start.5 = (f32[3,4,512]{2,1,0:T(4,128)}, f32[3,4,512]{2,1,0:T(4,128)S(1)}, u32[]{:S(2)}, u32[]{:S(2)}) collective-permute-start(f32[3,4,512]{2,1,0:T(4,128)} %get-tuple-element.8), channel_id=1, source_target_pairs={{4,0},{8,4},{12,8},{16,12},{20,16},{24,20},{28,24},{0,28},{5,1},{9... | collective-permute-start | bytes 73736 | tf_op jit(solution)/shard_map/ppermute | solution.py:270
  257.7 0.6 copy-start.3
  257.7 0.6 copy-start.4
